TPU v7x, 32 devices: a whole 2x2x4 slice. The times are simulated.
32 devices in a mesh: pipe: 2 (over x), expert: 16 (over z, y, core).
Axes of the slice: x: 2, y: 2, z: 4, core: 2. Of those that a mesh axis runs over, the one named last changes fastest.
Arguments:
- tokens: bfloat16 [2048, 1024], P('expert'), may hold values from -6 to 6
- out_grad: bfloat16 [2048, 1024], P('expert'), may hold values from -6 to 6
- routes: int32 [2048, 6], P('expert'), may hold values from 0 to 15, as said below
- slots: int32 [2048, 6], P('expert'), may hold values from 0 to 63, as said below
- gates: bfloat16 [2048, 6], P('expert'), may hold values from 0.099609375 to 1
- w_gate: bfloat16 [16, 1408, 1024], P('expert', 'pipe'), may hold values from -0.1875 to 0.1875
- w_up: bfloat16 [16, 1408, 1024], P('expert', 'pipe'), may hold values from -0.1875 to 0.1875
- w_down: bfloat16 [16, 1408, 1024], P('expert', 'pipe'), may hold values from -0.15625 to 0.15625
Outputs:
- mixed: bfloat16 [2048, 1024], P('expert', 'pipe')
- grad_tokens: bfloat16 [2048, 1024], P('expert', 'pipe')
- grad_gates: float32 [2048, 6], P('expert')
- grad_w_gate: bfloat16 [16, 1408, 1024], P('expert', 'pipe')
- grad_w_up: bfloat16 [16, 1408, 1024], P('expert', 'pipe')
- grad_w_down: bfloat16 [16, 1408, 1024], P('expert', 'pipe')
Inputs may be any that keep to these rules, and one draw needn't show every extreme that they name: `routes`: each token names 6 different experts. Within one device's block of 128 tokens no expert is named more than 64 times, and some expert is named exactly 64 times by every block. Within one block of 128 tokens the pairs (routes, slots) are all different.
All inputs are finite; a program needn't handle non-finite values.
Results may differ from a plain program's by a relative error of at most 0.015.
Values may be sent and summed in bfloat16 or wider, within the bound.
A program may use at most 64 MiB of HBM per device.

v0:
```python
import jax
import jax.numpy as jnp
from jax import lax
from jax.sharding import PartitionSpec as P


def expert_forward(arrived_x, gate_w, up_w, down_w):
    contract = (((1,), (1,)), ((), ()))
    gate_pre = lax.dot_general(arrived_x, gate_w, contract, preferred_element_type=jnp.float32)
    up_pre = lax.dot_general(arrived_x, up_w, contract, preferred_element_type=jnp.float32)
    sigma = jax.nn.sigmoid(gate_pre)
    silu_val = gate_pre * sigma
    act = (silu_val * up_pre).astype(jnp.bfloat16)
    partial_out = jnp.dot(act, down_w, preferred_element_type=jnp.float32).astype(jnp.bfloat16)
    return (partial_out, (gate_pre, up_pre, sigma, silu_val, act))


def expert_backward(arrived_x, arrived_dy, arrived_g, saved, gate_w, up_w, down_w):
    gate_pre, up_pre, sigma, silu_val, act = saved
    contract = (((1,), (1,)), ((), ()))
    over_rows = (((0,), (0,)), ((), ()))
    d_out = (arrived_g.astype(jnp.float32)[:, None] * arrived_dy.astype(jnp.float32)).astype(
        jnp.bfloat16
    )
    d_act = lax.dot_general(d_out, down_w, contract, preferred_element_type=jnp.float32)
    d_gate = (d_act * up_pre * sigma * (1.0 + gate_pre * (1.0 - sigma))).astype(jnp.bfloat16)
    d_up = (d_act * silu_val).astype(jnp.bfloat16)
    partial_back = (
        jnp.dot(d_gate, gate_w, preferred_element_type=jnp.float32)
        + jnp.dot(d_up, up_w, preferred_element_type=jnp.float32)
    ).astype(jnp.bfloat16)
    grad_gate_w = lax.dot_general(
        d_gate, arrived_x, over_rows, preferred_element_type=jnp.float32
    ).astype(jnp.bfloat16)
    grad_up_w = lax.dot_general(
        d_up, arrived_x, over_rows, preferred_element_type=jnp.float32
    ).astype(jnp.bfloat16)
    grad_down_w = lax.dot_general(act, d_out, over_rows, preferred_element_type=jnp.float32).astype(
        jnp.bfloat16
    )
    return (partial_back, (grad_gate_w[None], grad_up_w[None], grad_down_w[None]))


def pick_rows(returned, flat_slot, local_tokens, topk):
    slot_total = returned.shape[0] * returned.shape[1]
    flat_back = returned.reshape(slot_total, returned.shape[2])
    return jnp.take(flat_back, flat_slot, axis=0).reshape(local_tokens, topk, returned.shape[2])


def body(tokens, out_grad, routes, slots, gates, w_gate, w_up, w_down):
    local_tokens = tokens.shape[0]
    topk = routes.shape[1]
    sources = lax.axis_size("expert")
    experts = sources * w_gate.shape[0]
    capacity = 4 * local_tokens * topk // (3 * experts)
    slot_total = experts * capacity
    flat_slot = (routes * capacity + slots).reshape(-1)
    owner_token = jnp.arange(local_tokens * topk, dtype=jnp.int32) // topk
    owner = jnp.full((slot_total,), local_tokens, jnp.int32).at[flat_slot].set(owner_token)
    gate_slot = (
        jnp.zeros((slot_total,), jnp.bfloat16)
        .at[flat_slot]
        .set(gates.reshape(-1))
        .reshape(experts, capacity)
    )
    share = tokens.shape[1] // lax.axis_size("pipe")
    begin = lax.axis_index("pipe") * share

    def fill_rows(matrix):
        taken = jnp.take(matrix, owner, axis=0, mode="fill", fill_value=0)
        return taken.reshape(experts, capacity, matrix.shape[1])

    x_share = lax.dynamic_slice_in_dim(tokens, begin, share, 1)
    dy_share = lax.dynamic_slice_in_dim(out_grad, begin, share, 1)
    part_x, part_dy, arrived_g = (
        lax.all_to_all(fill_rows(x_share), "expert", split_axis=0, concat_axis=0, tiled=True),
        lax.all_to_all(fill_rows(dy_share), "expert", split_axis=0, concat_axis=0, tiled=True),
        lax.all_to_all(gate_slot, "expert", split_axis=0, concat_axis=0, tiled=True),
    )
    arrived_x, arrived_dy = (
        lax.all_gather(part_x, "pipe", axis=2, tiled=True),
        lax.all_gather(part_dy, "pipe", axis=2, tiled=True),
    )
    row_count = sources * capacity
    width = arrived_x.shape[2]
    arrived_x = arrived_x.reshape(row_count, width)
    arrived_dy = arrived_dy.reshape(row_count, width)
    arrived_g = arrived_g.reshape(row_count)
    gate_w = w_gate[0]
    up_w = w_up[0]
    down_w = w_down[0]
    ones_weight = jnp.ones((local_tokens, topk), jnp.bfloat16)
    batch_k = (((1,), (1,)), ((0,), (0,)))
    batch_d = (((2,), (1,)), ((0,), (0,)))
    partial_out, saved = expert_forward(arrived_x, gate_w, up_w, down_w)
    out_back = lax.all_to_all(
        partial_out.reshape(sources, capacity, width),
        "expert",
        split_axis=0,
        concat_axis=0,
        tiled=True,
    )
    picked = pick_rows(out_back, flat_slot, local_tokens, topk)
    mixed_part = lax.dot_general(gates, picked, batch_k, preferred_element_type=jnp.float32)
    gate_part = lax.dot_general(picked, out_grad, batch_d, preferred_element_type=jnp.float32)
    mixed_sum = lax.psum_scatter(
        mixed_part.astype(jnp.bfloat16), "pipe", scatter_dimension=1, tiled=True
    )
    partial_back, weight_grads = expert_backward(
        arrived_x, arrived_dy, arrived_g, saved, gate_w, up_w, down_w
    )
    grad_back = lax.all_to_all(
        partial_back.reshape(sources, capacity, width),
        "expert",
        split_axis=0,
        concat_axis=0,
        tiled=True,
    )
    picked_grad = pick_rows(grad_back, flat_slot, local_tokens, topk)
    grad_part = lax.dot_general(
        ones_weight, picked_grad, batch_k, preferred_element_type=jnp.float32
    )
    grad_total = lax.psum_scatter(
        grad_part.astype(jnp.bfloat16), "pipe", scatter_dimension=1, tiled=True
    )
    grad_gates = lax.psum(gate_part, "pipe")
    return (mixed_sum, grad_total, grad_gates, weight_grads[0], weight_grads[1], weight_grads[2])


def solution(mesh):
    return jax.shard_map(
        body,
        mesh=mesh,
        in_specs=(
            P("expert", None),
            P("expert", None),
            P("expert", None),
            P("expert", None),
            P("expert", None),
            P("expert", "pipe", None),
            P("expert", "pipe", None),
            P("expert", "pipe", None),
        ),
        out_specs=(
            P("expert", "pipe"),
            P("expert", "pipe"),
            P("expert", None),
            P("expert", "pipe", None),
            P("expert", "pipe", None),
            P("expert", "pipe", None),
        ),
        check_vma=False,
    )
```

profile of v0, /device:TPU:9, one launch (start us, length us, event | category | flops | bytes accessed | tf_op | source)
XLA Modules:
  0.0 285.5 jit_solution(10772181095873960082)
XLA Ops:
  8.3 3.4 %scatter_custom_fusion = s32[1024]{0:T(1024)S(1)} fusion(s32[768]{0:T(1024)S(1)} %fusion.23, s32[768]{0:T(1024)S(1)} %add_select_fusion, s32[]{:T(128)} %constant.34.clone.1), kind=kCustom, calls=%fused_computation.58 | custom fusion | bytes 4100 | tf_op jit(solution)/shard_map/scatter | solution.py:59
  12.8 4.0 %gather_fusion.2 = bf16[1024,512]{1,0:T(8,128)(2,1)S(1)} fusion(bf16[128,512]{1,0:T(8,128)(2,1)S(1)} %get-tuple-element.15, s32[1024]{0:T(1024)S(1)} %fusion.22), kind=kCustom, calls=%fused_computation.2.clone | custom fusion | bytes 2101248 | tf_op jit(solution)/shard_map/jit(_take)/gather | solution.py:70
  16.7 5.1 %gather_fusion = bf16[1024,512]{1,0:T(8,128)(2,1)} fusion(bf16[128,512]{1,0:T(8,128)(2,1)S(1)} %get-tuple-element.16, s32[1024]{0:T(1024)S(1)} %fusion.22), kind=kCustom, calls=%fused_computation.clone | custom fusion | bytes 2101248 | tf_op jit(solution)/shard_map/jit(_take)/gather | solution.py:70
  21.8 2.4 broadcast_select_fusion.2
  24.2 32.0 %all_to_all.30 = bf16[16,64,512]{2,1,0:T(8,128)(2,1)} all-to-all(bf16[16,64,512]{2,1,0:T(8,128)(2,1)S(1)} %bitcast.65), channel_id=1, replica_groups=mesh['pipe'=2,'expert'=16] {'expert'}, dimensions={0} | all-to-all | bytes 2097152 | tf_op jit(solution)/shard_map/all_to_all | solution.py:76
  56.3 29.6 %all_to_all.31 = bf16[16,64,512]{2,1,0:T(8,128)(2,1)} all-to-all(bf16[16,64,512]{2,1,0:T(8,128)(2,1)S(1)} %bitcast.64), channel_id=1, replica_groups=mesh['pipe'=2,'expert'=16] {'expert'}, dimensions={0} | all-to-all | bytes 2097152 | tf_op jit(solution)/shard_map/all_to_all | solution.py:77
  86.2 8.6 %scatter_custom_fusion.1 = bf16[1024]{0:T(1024)(128)(2,1)S(1)} fusion(s32[768]{0:T(1024)S(1)} %fusion.23, bf16[768]{0:T(1024)(128)(2,1)S(1)} %reshape.169, bf16[]{:T(256)} %constant.22.clone.1), kind=kCustom, calls=%fused_computation.60 | custom fusion | bytes 2050 | tf_op jit(solution)/shard_map/scatter | solution.py:63
  94.9 8.9 %all_to_all.32 = bf16[16,1,64]{2,1,0:T(2,128)(2,1)S(1)} all-to-all(bf16[16,1,64]{2,1,0:T(2,128)(2,1)S(1)} %all_to_all.24), channel_id=1, replica_groups=mesh['pipe'=2,'expert'=16] {'expert'}, dimensions={0} | all-to-all | bytes 4096 | tf_op jit(solution)/shard_map/all_to_all | solution.py:78
  103.9 5.4 %fusion.9 = f32[1024,704]{0,1:T(8,128)} fusion(bf16[1024,1024]{1,0:T(8,128)(2,1)} %bitcast.75, bf16[1,704,1024]{2,1,0:T(8,128)(2,1)} %param.18), kind=kOutput, calls=%fused_computation.28 | convolution fusion | flops 1476395008 | bytes 6422528 | tf_op jit(solution)/shard_map/dot_general | solution.py:10
  109.3 3.3 %fusion.13 = f32[1024,704]{0,1:T(8,128)} fusion(bf16[1024,1024]{1,0:T(8,128)(2,1)S(1)} %bitcast.77, bf16[1,704,1024]{2,1,0:T(8,128)(2,1)S(1)} %copy-done.9), kind=kOutput, calls=%fused_computation.32 | convolution fusion | flops 1476395008 | bytes 6422528 | tf_op jit(solution)/shard_map/dot_general | solution.py:9
  112.6 10.4 %all-gather.5.cloned.1.call-done = bf16[16,64,1024]{2,1,0:T(8,128)(2,1)} async-done(((bf16[16,64,512]{2,1,0:T(8,128)(2,1)}), bf16[16,64,1024]{2,1,0:T(8,128)(2,1)}) %all-gather.5.cloned.1.call-update) | async-done | bytes 2097168 | tf_op jit(solution)/shard_map/all_gather | solution.py:82
  123.0 2.1 multiply_convert_fusion
  125.4 5.4 %multiply_convert_fusion.1 = (bf16[1024,704]{0,1:T(8,128)(2,1)}, bf16[1024,704]{0,1:T(8,128)(2,1)}, bf16[1024,704]{0,1:T(8,128)(2,1)S(1)}) fusion(f32[1024,704]{0,1:T(8,128)} %fusion.13, f32[1024,704]{0,1:T(8,128)S(1)} %copy-done.11, bf16[1024,1024]{1,0:T(8,128)(2,1)S(1)} %bitcast.68, bf16[1,704,1024]{2,1,0:T(8,128)(2,1)S(1)} %copy-done), kind=kOutput, calls=%fused_computation.10 | convolution fusion | flops 1487208448 | bytes 13631488 | tf_op jit(solution)/shard_map/dot_general | solution.py:25
  130.8 3.2 %convolution_convert_fusion = bf16[1024,1024]{1,0:T(8,128)(2,1)} fusion(bf16[1024,704]{0,1:T(8,128)(2,1)S(1)} %get-tuple-element.10, bf16[1,704,1024]{2,1,0:T(8,128)(2,1)S(1)} %copy-done), kind=kOutput, calls=%fused_computation.15 | convolution fusion | flops 1477443584 | bytes 4980736 | tf_op jit(solution)/shard_map/dot_general | solution.py:14
  134.0 6.5 %all-to-all-start.1 = ((bf16[16,64,1024]{2,1,0:T(8,128)(2,1)}), bf16[16,64,1024]{2,1,0:T(8,128)(2,1)S(1)}, u32[]{:S(2)}, u32[]{:S(2)}) async-start(bf16[16,64,1024]{2,1,0:T(8,128)(2,1)} %bitcast.67), calls=%async_computation.1 | async-start | bytes 4194304 | tf_op jit(solution)/shard_map/all_to_all | solution.py:96
  140.5 3.8 %fusion.11 = f32[1024,1024]{1,0:T(8,128)S(1)} fusion(bf16[1024,704]{0,1:T(8,128)(2,1)} %get-tuple-element.9, bf16[1,704,1024]{2,1,0:T(8,128)(2,1)} %param.17), kind=kOutput, calls=%fused_computation.30 | convolution fusion | flops 1476395008 | bytes 7077888 | tf_op jit(solution)/shard_map/dot_general | solution.py:29
  144.4 3.3 %add_convert_fusion = bf16[1024,1024]{1,0:T(8,128)(2,1)} fusion(f32[1024,1024]{1,0:T(8,128)S(1)} %fusion.11, bf16[1024,704]{0,1:T(8,128)(2,1)S(1)} %copy-done.13, bf16[1,704,1024]{2,1,0:T(8,128)(2,1)S(1)} %copy-done.10), kind=kOutput, calls=%fused_computation.8 | convolution fusion | flops 1478492160 | bytes 9175040 | tf_op jit(solution)/shard_map/dot_general | solution.py:30
  147.7 38.9 %all-to-all-done.1 = bf16[16,64,1024]{2,1,0:T(8,128)(2,1)S(1)} async-done(((bf16[16,64,1024]{2,1,0:T(8,128)(2,1)}), bf16[16,64,1024]{2,1,0:T(8,128)(2,1)S(1)}, u32[]{:S(2)}, u32[]{:S(2)}) %all-to-all-start.1) | async-done | bytes 2097184 | tf_op jit(solution)/shard_map/all_to_all | solution.py:96
  186.6 6.1 %all-to-all-start.4 = ((bf16[16,64,1024]{2,1,0:T(8,128)(2,1)}), bf16[16,64,1024]{2,1,0:T(8,128)(2,1)}, u32[]{:S(2)}, u32[]{:S(2)}) async-start(bf16[16,64,1024]{2,1,0:T(8,128)(2,1)} %bitcast.66), calls=%async_computation.5 | async-start | bytes 4194304 | tf_op jit(solution)/shard_map/all_to_all | solution.py:112
  196.7 4.9 %fusion.3 = bf16[1,704,1024]{2,1,0:T(8,128)(2,1)} fusion(bf16[1024,704]{0,1:T(8,128)(2,1)} %get-tuple-element.8, bf16[1024,1024]{1,0:T(8,128)(2,1)} %bitcast.76), kind=kOutput, calls=%fused_computation.22 | convolution fusion | flops 1477115904 | bytes 4980736 | tf_op jit(solution)/shard_map/dot_general | solution.py:35
  201.6 2.8 fusion.2
  204.4 3.6 %gather_fusion.1 = bf16[768,1024]{1,0:T(8,128)(2,1)} fusion(bf16[1024,1024]{1,0:T(8,128)(2,1)S(1)} %bitcast.63, s32[1024]{0:T(1024)S(1)} %pad_clamp_fusion), kind=kCustom, calls=%fused_computation.1.clone | custom fusion | bytes 3148800 | tf_op jit(solution)/shard_map/jit(_take)/gather | solution.py:47
  208.0 30.9 %all-to-all-done.4 = bf16[16,64,1024]{2,1,0:T(8,128)(2,1)} async-done(((bf16[16,64,1024]{2,1,0:T(8,128)(2,1)}), bf16[16,64,1024]{2,1,0:T(8,128)(2,1)}, u32[]{:S(2)}, u32[]{:S(2)}) %all-to-all-start.4) | async-done | bytes 2097184 | tf_op jit(solution)/shard_map/all_to_all | solution.py:112
  238.9 6.6 %gather_fusion.3 = bf16[768,1024]{1,0:T(8,128)(2,1)} fusion(bf16[1024,1024]{1,0:T(8,128)(2,1)} %bitcast.13, s32[1024]{0:T(1024)S(1)} %pad_clamp_fusion), kind=kCustom, calls=%fused_computation.3.clone | custom fusion | bytes 3148800 | tf_op jit(solution)/shard_map/jit(_take)/gather | solution.py:47
  245.5 3.5 %broadcast_select_fusion = (bf16[768,1024]{1,0:T(8,128)(2,1)}, bf16[768,1024]{1,0:T(8,128)(2,1)}) fusion(bf16[768,1024]{1,0:T(8,128)(2,1)} %gather_fusion.3, pred[768]{0:T(1024)(128)(4,1)S(1)} %copy-done.6, bf16[768,1024]{1,0:T(8,128)(2,1)S(1)} %copy-done.1), kind=kLoop, calls=%fused_computation.19 | loop fusion | flops 1572864 | bytes 6292224 | tf_op jit(solution)/shard_map/jit(_take)/select_n | solution.py:47
  249.0 2.5 reshape.121
  253.0 3.3 %fusion = bf16[1024,1024]{1,0:T(8,128)(2,1)} fusion(f32[1024]{0:T(1024)S(1)} %reshape.123, bf16[16,64,1024]{2,1,0:T(8,128)(2,1)} %all-gather.5.cloned.1.call-done), kind=kLoop, calls=%fused_computation.7 | loop fusion | flops 3145728 | bytes 4198400 | tf_op jit(solution)/shard_map/convert_element_type | solution.py:22
  256.4 2.5 reshape.116
  261.2 4.8 %fusion.4 = bf16[1,704,1024]{2,1,0:T(8,128)(2,1)} fusion(bf16[1024,704]{0,1:T(8,128)(2,1)} %copy-done.14, bf16[1024,1024]{1,0:T(8,128)(2,1)} %fusion), kind=kOutput, calls=%fused_computation.23 | convolution fusion | flops 1477115904 | bytes 4980736 | tf_op jit(solution)/shard_map/dot_general | solution.py:38
  266.1 2.1 fusion.15
  269.0 4.4 %psum.7 = f32[128,6]{0,1:T(8,128)} all-reduce(f32[128,6]{0,1:T(8,128)S(1)} %bitcast.73), channel_id=1, replica_groups=mesh['pipe'=2,'expert'=16] {'pipe'}, use_global_device_ids=true, to_apply=%region_4.7 | all-reduce | flops 768 | bytes 6144 | tf_op jit(solution)/shard_map/psum | solution.py:126
  273.4 5.6 %reduce-scatter.3.cloned.1.call-done = bf16[128,512]{1,0:T(8,128)(2,1)} async-done(((bf16[128,1024]{1,0:T(8,128)(2,1)}), bf16[128,512]{1,0:T(8,128)(2,1)}) %reduce-scatter.3.cloned.1.call-update) | async-done | bytes 131088 | tf_op jit(solution)/shard_map/reduce_scatter | solution.py:106
  (64 shorter events, 11.7 us)
Async XLA Ops:
  7.2 117.9 %copy-start = (bf16[1,704,1024]{2,1,0:T(8,128)(2,1)S(1)}, bf16[1,704,1024]{2,1,0:T(8,128)(2,1)}, u32[]{:S(2)}) copy-start(bf16[1,704,1024]{2,1,0:T(8,128)(2,1)} %param.19) | copy-start | bytes 4325380
  7.2 96.7 %all-gather.3.cloned.1.call-start = ((), (), s32[]{:S(2)}) async-start(), calls=%async_computation.7 | async-start | bytes 3145728 | tf_op jit(solution)/shard_map/all_gather | solution.py:81
  8.2 3.6 %copy-start.3 = (s32[128,6]{1,0:T(8,128)}, s32[128,6]{1,0:T(8,128)S(1)}, u32[]{:S(2)}) copy-start(s32[128,6]{1,0:T(8,128)S(1)} %copy.20) | copy-start | bytes 9220
  24.2 32.0 %copy-start.2 = (bf16[1024,512]{1,0:T(8,128)(2,1)S(1)}, bf16[1024,512]{1,0:T(8,128)(2,1)}, u32[]{:S(2)}) copy-start(bf16[1024,512]{1,0:T(8,128)(2,1)} %get-tuple-element.13) | copy-start | bytes 3145732
  56.2 29.7 %copy-start.5 = (bf16[128,6]{0,1:T(8,128)(2,1)S(1)}, bf16[128,6]{0,1:T(8,128)(2,1)}, u32[]{:S(2)}) copy-start(bf16[128,6]{0,1:T(8,128)(2,1)} %param.16) | copy-start | bytes 4612
  56.2 66.7 %all-gather.5.cloned.1.call-start = ((), (), s32[]{:S(2)}) async-start(), calls=%async_computation.9 | async-start | bytes 3145728 | tf_op jit(solution)/shard_map/all_gather | solution.py:82
  103.9 5.5 %copy-start.7 = (bf16[16,64,1024]{2,1,0:T(8,128)(2,1)S(1)}, bf16[16,64,1024]{2,1,0:T(8,128)(2,1)}, u32[]{:S(2)}) copy-start(bf16[16,64,1024]{2,1,0:T(8,128)(2,1)} %all-gather.3.cloned.1.call-done) | copy-start | bytes 6291460
  103.9 5.5 %copy-start.9 = (bf16[1,704,1024]{2,1,0:T(8,128)(2,1)S(1)}, bf16[1,704,1024]{2,1,0:T(8,128)(2,1)}, u32[]{:S(2)}) copy-start(bf16[1,704,1024]{2,1,0:T(8,128)(2,1)} %param.17) | copy-start | bytes 4325380
  123.0 2.4 copy-start.11
  130.8 3.2 %copy-start.14 = (bf16[1024,704]{0,1:T(8,128)(2,1)}, bf16[1024,704]{0,1:T(8,128)(2,1)S(1)}, u32[]{:S(2)}) copy-start(bf16[1024,704]{0,1:T(8,128)(2,1)S(1)} %get-tuple-element.10) | copy-start | bytes 4325380
  134.0 52.6 %all-to-all-start.1 = ((bf16[16,64,1024]{2,1,0:T(8,128)(2,1)}), bf16[16,64,1024]{2,1,0:T(8,128)(2,1)S(1)}, u32[]{:S(2)}, u32[]{:S(2)}) async-start(bf16[16,64,1024]{2,1,0:T(8,128)(2,1)} %bitcast.67), calls=%async_computation.1 | async-start | bytes 4194304 | tf_op jit(solution)/shard_map/all_to_all | solution.py:96
  140.5 3.8 %copy-start.10 = (bf16[1,704,1024]{2,1,0:T(8,128)(2,1)S(1)}, bf16[1,704,1024]{2,1,0:T(8,128)(2,1)}, u32[]{:S(2)}) copy-start(bf16[1,704,1024]{2,1,0:T(8,128)(2,1)} %param.18) | copy-start | bytes 4325380
  140.5 3.8 %copy-start.13 = (bf16[1024,704]{0,1:T(8,128)(2,1)S(1)}, bf16[1024,704]{0,1:T(8,128)(2,1)}, u32[]{:S(2)}) copy-start(bf16[1024,704]{0,1:T(8,128)(2,1)} %get-tuple-element.8) | copy-start | bytes 4325380
  186.6 52.3 %all-to-all-start.4 = ((bf16[16,64,1024]{2,1,0:T(8,128)(2,1)}), bf16[16,64,1024]{2,1,0:T(8,128)(2,1)}, u32[]{:S(2)}, u32[]{:S(2)}) async-start(bf16[16,64,1024]{2,1,0:T(8,128)(2,1)} %bitcast.66), calls=%async_computation.5 | async-start | bytes 4194304 | tf_op jit(solution)/shard_map/all_to_all | solution.py:112
  192.7 80.7 %reduce-scatter.5.cloned.1.call-start = ((), (), s32[]{:S(2)}) async-start(), calls=%async_computation.10 | async-start | bytes 393216 | tf_op jit(solution)/shard_map/reduce_scatter | solution.py:123
  196.7 4.9 %copy-start.8 = (bf16[16,64,1024]{2,1,0:T(8,128)(2,1)S(1)}, bf16[16,64,1024]{2,1,0:T(8,128)(2,1)}, u32[]{:S(2)}) copy-start(bf16[16,64,1024]{2,1,0:T(8,128)(2,1)} %all-gather.3.cloned.1.call-done) | copy-start | bytes 6291460
  196.7 4.9 %copy-start.12 = (bf16[1024,704]{0,1:T(8,128)(2,1)S(1)}, bf16[1024,704]{0,1:T(8,128)(2,1)}, u32[]{:S(2)}) copy-start(bf16[1024,704]{0,1:T(8,128)(2,1)} %get-tuple-element.9) | copy-start | bytes 4325380
  238.9 6.6 %copy-start.1 = (bf16[768,1024]{1,0:T(8,128)(2,1)S(1)}, bf16[768,1024]{1,0:T(8,128)(2,1)}, u32[]{:S(2)}) copy-start(bf16[768,1024]{1,0:T(8,128)(2,1)} %gather_fusion.1) | copy-start | bytes 4718596
  238.9 6.6 %copy-start.6 = (pred[768]{0:T(1024)(128)(4,1)S(1)}, pred[768]{0:T(1024)(128)(4,1)}, u32[]{:S(2)}) copy-start(pred[768]{0:T(1024)(128)(4,1)} %compare_and_fusion) | copy-start | bytes 2308
  253.0 26.0 %reduce-scatter.3.cloned.1.call-start = ((), (), s32[]{:S(2)}) async-start(), calls=%async_computation.8 | async-start | bytes 393216 | tf_op jit(solution)/shard_map/reduce_scatter | solution.py:106
  261.2 4.9 %copy-start.4 = (bf16[128,1024]{1,0:T(8,128)(2,1)S(1)}, bf16[128,1024]{1,0:T(8,128)(2,1)}, u32[]{:S(2)}) copy-start(bf16[128,1024]{1,0:T(8,128)(2,1)} %param.13) | copy-start | bytes 786436
Sparse Core Ops, SparseCore 0:
  56.3 31.8 all-gather.2
  89.8 33.0 all-gather.4
  253.1 11.3 reduce-scatter.4
  267.2 11.7 reduce-scatter.2
where the time goes:
time: 288 us; the launch traced here: 286 us
  waiting for transfers between devices  85.8 us (30%)
  blocking collectives  74.8 us (26%)
  local copies, waits for them, and re-layouts  43.1 us (15%)
  matrix products  41.3 us (14%)
  between operations  14 us (5%)
  other arithmetic  13.5 us (5%)
  starting transfers between devices  13 us (5%)
    all_to_all x1, waiting for transfers between devices, body(): lax.all_to_all(partial_out.reshape(sources, capacity, width), 'expert', s...  38.9 us
    all_to_all x1, blocking collectives, body(): lax.all_to_all(fill_rows(x_share), 'expert', split_axis=0, concat_axis=0,...  32 us
    all_to_all x1, waiting for transfers between devices, body(): lax.all_to_all(partial_back.reshape(sources, capacity, width), 'expert',...  30.9 us
    all_to_all x1, blocking collectives, body(): lax.all_to_all(fill_rows(dy_share), 'expert', split_axis=0, concat_axis=0...  29.6 us
    all_gather x1, waiting for transfers between devices, body(): lax.all_gather(part_dy, 'pipe', axis=2, tiled=True)  10.4 us
    gather x2, local copies, waits for them, and re-layouts, pick_rows(): jnp.take(flat_back, flat_slot, axis=0)  10.1 us
    gather x2, local copies, waits for them, and re-layouts, fill_rows(): taken = jnp.take(matrix, owner, axis=0, mode='fill', fill_value=0)  9.05 us
    all_to_all x1, blocking collectives, body(): lax.all_to_all(gate_slot, 'expert', split_axis=0, concat_axis=0, tiled=True)  8.9 us
  transfers between devices with their start and end apart: 6, of which 4 were waited for; matrix products, arithmetic and copies ran while one was open for 20% of the time, Pallas kernels for 0%

commit v1 on v0

v1 whole, which is shorter than its diff:
```python
import functools

import jax
import jax.numpy as jnp
from jax import lax
from jax.experimental import pallas as pl
from jax.experimental.pallas import tpu as pltpu
from jax.sharding import PartitionSpec as P

INNER = 2
BF16 = jnp.bfloat16
F32 = jnp.float32


def place(experts):
    me = lax.axis_index("expert")
    return me, me // (INNER * INNER), (me // INNER) % INNER, me % INNER


def join(outer, mid, low):
    return (outer * INNER + mid) * INNER + low


def peer(expert=None, pipe=None):
    p = lax.axis_index("pipe") if pipe is None else pipe
    e = lax.axis_index("expert") if expert is None else expert
    return (p, e)


def meet(pipes, experts):
    p = lax.axis_index("pipe")
    e = lax.axis_index("expert")
    barrier = pltpu.get_barrier_semaphore()
    for d in range(1, experts):
        pl.semaphore_signal(barrier, inc=1, device_id=peer(expert=(e + d) % experts),
                            device_id_type=pl.DeviceIdType.MESH)
    for d in range(1, pipes):
        pl.semaphore_signal(barrier, inc=1, device_id=peer(pipe=(p + d) % pipes),
                            device_id_type=pl.DeviceIdType.MESH)
    pl.semaphore_wait(barrier, experts + pipes - 2)


def remote(src, dst, send, recv, dev):
    return pltpu.make_async_remote_copy(src_ref=src, dst_ref=dst, send_sem=send, recv_sem=recv,
                                        device_id=dev, device_id_type=pl.DeviceIdType.MESH)


def gather_plan(pipes, experts):
    outer = experts // (INNER * INNER)
    lanes = 2 * outer - 1
    base = {"z": 0, "y": outer - 1, "own": 2 * outer - 1, "c": 2 * outer, "x": 2 * outer + lanes}
    base["cx"] = base["x"] + lanes
    return outer, lanes, base, base["cx"] + lanes


def gather_kernel(pipes, experts, x, dy, meta, xg, dyg, mg, send, recv, msend, mrecv, local):
    me, z, y, c = place(experts)
    p = lax.axis_index("pipe")
    outer, lanes, base, count = gather_plan(pipes, experts)
    width = x.shape[1]
    side = (width // 128 * 3 // 8) * 128
    par = p % 2
    wide = pl.ds(pl.multiple_of(par * side, 128), width - side)
    give = pl.ds(pl.multiple_of(par * (width - side), 128), side)
    take = pl.ds(pl.multiple_of((1 - par) * (width - side), 128), side)
    xpeer = peer(pipe=p + 1 - 2 * par)
    cpeer = peer(expert=join(z, y, 1 - c))
    ypeer = peer(expert=join(z, 1 - y, c))
    own = [pltpu.make_async_copy(s, g.at[me], local.at[i])
           for i, (s, g) in enumerate(((x, xg), (dy, dyg), (meta, mg)))]
    for copy in own:
        copy.start()
    meet(pipes, experts)
    sent = []

    def go(src, dst, s, r, dev):
        copy = remote(src, dst, s, r, dev)
        copy.start()
        sent.append(copy)

    for d in range(1, experts):
        go(meta, mg.at[me], msend.at[d - 1], mrecv.at[d - 1], peer(expert=(me + d) % experts))
    arrays = ((x, xg), (dy, dyg))

    def sems(a, i):
        return send.at[a * count + i], recv.at[a * count + i]

    def arrived(ref, a, i):
        remote(ref, ref, *sems(a, i), cpeer).wait_recv()

    for a, (s, g) in enumerate(arrays):
        for d in range(1, outer):
            go(s.at[:, wide], g.at[me, :, wide], *sems(a, base["z"] + d - 1),
               peer(expert=join((z + d) % outer, y, c)))
        go(s.at[:, wide], g.at[me, :, wide], *sems(a, base["y"]), ypeer)
        go(s, g.at[me], *sems(a, base["own"]), cpeer)
    for a, (s, g) in enumerate(arrays):
        for d in range(1, outer):
            b = join((z + outer - d) % outer, y, c)
            arrived(g.at[b, :, wide], a, base["z"] + d - 1)
            go(g.at[b, :, wide], g.at[b, :, wide], *sems(a, base["y"] + d), ypeer)
            go(g.at[b, :, give], g.at[b, :, give], *sems(a, base["x"] + d - 1), xpeer)
            go(g.at[b, :, wide], g.at[b, :, wide], *sems(a, base["c"] + d - 1), cpeer)
        for d in range(outer):
            b = join((z + outer - d) % outer, 1 - y, c)
            arrived(g.at[b, :, wide], a, base["y"] + d)
            go(g.at[b, :, give], g.at[b, :, give], *sems(a, base["x"] + outer - 1 + d), xpeer)
            go(g.at[b, :, wide], g.at[b, :, wide], *sems(a, base["c"] + outer - 1 + d), cpeer)
    for a, (s, g) in enumerate(arrays):
        for i in range(lanes):
            b = (join((z + outer - i - 1) % outer, y, c) if i < outer - 1
                 else join((z + outer - (i - outer + 1)) % outer, 1 - y, c))
            arrived(g.at[b, :, take], a, base["x"] + i)
            go(g.at[b, :, take], g.at[b, :, take], *sems(a, base["cx"] + i), cpeer)
    for a, (s, g) in enumerate(arrays):
        arrived(g.at[join(z, y, 1 - c)], a, base["own"])
        for i in range(lanes):
            b = (join((z + outer - i - 1) % outer, y, 1 - c) if i < outer - 1
                 else join((z + outer - (i - outer + 1)) % outer, 1 - y, 1 - c))
            arrived(g.at[b, :, wide], a, base["c"] + i)
            arrived(g.at[b, :, take], a, base["cx"] + i)
    for d in range(1, experts):
        b = (me + experts - d) % experts
        remote(mg.at[b], mg.at[b], msend.at[d - 1], mrecv.at[d - 1], cpeer).wait_recv()
    for copy in sent:
        copy.wait_send()
    for copy in own:
        copy.wait()


def gather_all(pipes, experts, x, dy, meta):
    count = gather_plan(pipes, experts)[3]
    hbm = pl.BlockSpec(memory_space=pl.ANY)
    vmem = pl.BlockSpec(memory_space=pltpu.VMEM)
    return pl.pallas_call(
        functools.partial(gather_kernel, pipes, experts),
        out_shape=[jax.ShapeDtypeStruct((experts,) + v.shape, v.dtype) for v in (x, dy, meta)],
        in_specs=[vmem] * 3,
        out_specs=[hbm] * 3,
        scratch_shapes=[
            pltpu.SemaphoreType.DMA((2 * count,)),
            pltpu.SemaphoreType.DMA((2 * count,)),
            pltpu.SemaphoreType.DMA((experts - 1,)),
            pltpu.SemaphoreType.DMA((experts - 1,)),
            pltpu.SemaphoreType.DMA((3,)),
        ],
        compiler_params=pltpu.CompilerParams(collective_id=0, has_side_effects=True),
        name="gather_rows",
    )(x, dy, meta)


def reduce_plan(pipes, experts):
    outer = experts // (INNER * INNER)
    groups = min(outer, 4)
    chunks = 2 * groups
    base = {"c": 0, "x": chunks, "y": chunks * pipes}
    base["z"] = base["y"] + groups
    return outer, groups, base, base["z"] + outer - 1


def reduce_kernel(pipes, experts, pm, pg, gate, om, og, ogate,
                  stay, come, xin, half, yin, line, zin, gin, gx,
                  send, recv, gsend, grecv, gxs, gxr, local):
    me, z, y, c = place(experts)
    p = lax.axis_index("pipe")
    outer, groups, base, count = reduce_plan(pipes, experts)
    size = outer // groups
    chunks = 2 * groups
    share = om.shape[1]
    cpeer = peer(expert=join(z, y, 1 - c))
    ypeer = peer(expert=join(z, 1 - y, c))
    mine = pl.ds(pl.multiple_of(p * share, 128), share)
    parts = (pm, pg)
    outs = (om, og)

    def where(k):
        g = (z // size + 1 + k % groups) % groups
        return (y + 1 + k // groups) % 2, pl.ds(g * size, size)

    def where_peer(k):
        return where(k)

    loads = []
    for a in range(2):
        for k in range(chunks):
            yy, zz = where(k)
            copy = pltpu.make_async_copy(parts[a].at[zz, yy, c], stay.at[a, yy, zz],
                                         local.at[a * chunks + k])
            copy.start()
            loads.append(copy)
    keep = pltpu.make_async_copy(gate.at[me], gin.at[me], local.at[2 * chunks])
    keep.start()
    meet(pipes, experts)
    sent = []

    def sems(a, i):
        return send.at[a * count + i], recv.at[a * count + i]

    def go(src, dst, s, r, dev):
        copy = remote(src, dst, s, r, dev)
        copy.start()
        sent.append(copy)

    def arrived(ref, a, i):
        remote(ref, ref, *sems(a, i), cpeer).wait_recv()

    for d in range(1, experts):
        to = (me + d) % experts
        go(gate.at[to], gin.at[me], gsend.at[d - 1], grecv.at[d - 1], peer(expert=to))
    for a in range(2):
        for k in range(chunks):
            yy, zz = where(k)
            go(parts[a].at[zz, yy, 1 - c], come.at[a, yy, zz], *sems(a, base["c"] + k), cpeer)

    def core_step(a, k):
        yy, zz = where(k)
        loads[a * chunks + k].wait()
        arrived(come.at[a, yy, zz], a, base["c"] + k)
        stay[a, yy, zz] = (stay[a, yy, zz].astype(F32) + come[a, yy, zz].astype(F32)).astype(BF16)
        for j in range(1, pipes):
            to = (p + j) % pipes
            cols = pl.ds(pl.multiple_of(to * share, 128), share)
            go(stay.at[a, yy, zz, :, cols], xin.at[a, j - 1, yy, zz],
               *sems(a, base["x"] + (j - 1) * chunks + k), peer(pipe=to))

    def x_step(a, k):
        yy, zz = where(k)
        total = stay[a, yy, zz, :, mine].astype(F32)
        for j in range(1, pipes):
            arrived(xin.at[a, j - 1, yy, zz], a, base["x"] + (j - 1) * chunks + k)
            total = total + xin[a, j - 1, yy, zz].astype(F32)
        half[a, yy, zz] = total.astype(BF16)
        if k < groups:
            go(half.at[a, yy, zz], yin.at[a, zz], *sems(a, base["y"] + k), ypeer)

    def y_step(a, k):
        yy, zz = where(groups + k)
        arrived(yin.at[a, zz], a, base["y"] + k)
        line[a, zz] = (half[a, yy, zz].astype(F32) + yin[a, zz].astype(F32)).astype(BF16)
        if size == 1 and k < groups - 1:
            z_send(a, k + 1)

    def z_send(a, d):
        to = (z + d) % outer
        go(line.at[a, to], zin.at[a, d - 1], *sems(a, base["z"] + d - 1),
           peer(expert=join(to, y, c)))

    for a in range(2):
        for k in range(chunks):
            core_step(a, k)
    for d in range(1, experts):
        b = (me + experts - d) % experts
        remote(gin.at[b], gin.at[b], gsend.at[d - 1], grecv.at[d - 1], cpeer).wait_recv()
    keep.wait()
    for j in range(1, pipes):
        go(gin, gx.at[j - 1], gxs.at[j - 1], gxr.at[j - 1], peer(pipe=(p + j) % pipes))
    for a in range(2):
        for k in range(chunks):
            x_step(a, k)
        for k in range(groups):
            y_step(a, k)
        if size > 1:
            for d in range(1, outer):
                z_send(a, d)
    whole = gin[...]
    for j in range(1, pipes):
        remote(gin, gx.at[j - 1], gxs.at[j - 1], gxr.at[j - 1], cpeer).wait_recv()
        whole = whole + gx[j - 1]
    ogate[...] = whole
    for a in range(2):
        total = line[a, z].astype(F32)
        for d in range(1, outer):
            arrived(zin.at[a, d - 1], a, base["z"] + d - 1)
            total = total + zin[a, d - 1].astype(F32)
        outs[a][...] = total.astype(BF16)
    for copy in sent:
        copy.wait_send()


def reduce_all(pipes, experts, mixed, grad, gate):
    outer, groups, base, count = reduce_plan(pipes, experts)
    rows, width = mixed.shape[1:]
    share = width // pipes
    shape = (outer, INNER, INNER, rows, width)
    hbm = pl.BlockSpec(memory_space=pl.ANY)
    vmem = pl.BlockSpec(memory_space=pltpu.VMEM)
    return pl.pallas_call(
        functools.partial(reduce_kernel, pipes, experts),
        out_shape=[jax.ShapeDtypeStruct((rows, share), BF16)] * 2
        + [jax.ShapeDtypeStruct(gate.shape, F32)],
        in_specs=[hbm, hbm, vmem],
        out_specs=[vmem] * 3,
        scratch_shapes=[
            pltpu.VMEM((2, INNER, outer, rows, width), BF16),
            pltpu.VMEM((2, INNER, outer, rows, width), BF16),
            pltpu.VMEM((2, pipes - 1, INNER, outer, rows, share), BF16),
            pltpu.VMEM((2, INNER, outer, rows, share), BF16),
            pltpu.VMEM((2, outer, rows, share), BF16),
            pltpu.VMEM((2, outer, rows, share), BF16),
            pltpu.VMEM((2, outer - 1, rows, share), BF16),
            pltpu.VMEM(gate.shape, F32),
            pltpu.VMEM((pipes - 1,) + gate.shape, F32),
            pltpu.SemaphoreType.DMA((2 * count,)),
            pltpu.SemaphoreType.DMA((2 * count,)),
            pltpu.SemaphoreType.DMA((experts - 1,)),
            pltpu.SemaphoreType.DMA((experts - 1,)),
            pltpu.SemaphoreType.DMA((pipes - 1,)),
            pltpu.SemaphoreType.DMA((pipes - 1,)),
            pltpu.SemaphoreType.DMA((4 * groups + 1,)),
        ],
        compiler_params=pltpu.CompilerParams(collective_id=1, has_side_effects=True),
        name="reduce_rows",
    )(mixed.reshape(shape), grad.reshape(shape), gate)


def body(tokens, out_grad, routes, slots, gates, w_gate, w_up, w_down):
    local_tokens, topk = routes.shape
    pipes = lax.axis_size("pipe")
    experts = lax.axis_size("expert")
    capacity = 4 * local_tokens * topk // (3 * experts)
    width = tokens.shape[1]
    half = (topk + 7) // 8 * 8
    position = (routes * capacity + slots).astype(F32)
    pad = jnp.zeros((local_tokens, half - topk), F32)
    meta = jnp.concatenate([position, pad, gates.astype(F32), pad], axis=1).T
    xg, dyg, mg = gather_all(pipes, experts, tokens, out_grad, meta)

    rows = experts * capacity
    first = lax.axis_index("expert") * capacity
    wanted = (first + jnp.arange(capacity)).astype(F32)
    hit = mg[:, :topk, None, :] == wanted[None, None, :, None]
    pick = jnp.sum(hit.astype(F32), axis=1).astype(BF16)
    weigh = jnp.sum(jnp.where(hit, mg[:, half:half + topk, None, :], 0.0), axis=1).astype(BF16)
    by_token = (((2,), (1,)), ((0,), (0,)))

    def select(matrix, source):
        picked = lax.dot_general(matrix, source, by_token, preferred_element_type=F32)
        return picked.astype(BF16).reshape(rows, width)

    x = select(pick, xg)
    dy = select(pick, dyg)
    d_out = select(weigh, dyg)
    gate_w, up_w, down_w = w_gate[0], w_up[0], w_down[0]
    contract = (((1,), (1,)), ((), ()))
    over_rows = (((0,), (0,)), ((), ()))
    dot = functools.partial(lax.dot_general, preferred_element_type=F32)
    plain = (((1,), (0,)), ((), ()))
    gate_pre = dot(x, gate_w, contract)
    up_pre = dot(x, up_w, contract)
    sigma = jax.nn.sigmoid(gate_pre)
    silu_val = gate_pre * sigma
    act = (silu_val * up_pre).astype(BF16)
    partial_out = dot(act, down_w, plain).astype(BF16)
    d_act = dot(d_out, down_w, contract)
    d_gate = (d_act * up_pre * sigma * (1.0 + gate_pre * (1.0 - sigma))).astype(BF16)
    d_up = (d_act * silu_val).astype(BF16)
    partial_back = (dot(d_gate, gate_w, plain) + dot(d_up, up_w, plain)).astype(BF16)
    grad_gate_w = dot(d_gate, x, over_rows).astype(BF16)
    grad_up_w = dot(d_up, x, over_rows).astype(BF16)
    grad_down_w = dot(act, d_out, over_rows).astype(BF16)

    over_slots = (((1,), (1,)), ((0,), (0,)))
    shape = (experts, capacity, width)
    mixed_part = dot(weigh, partial_out.reshape(shape), over_slots).astype(BF16)
    grad_part = dot(pick, partial_back.reshape(shape), over_slots).astype(BF16)
    row_gate = jnp.sum(dy.astype(F32) * partial_out.astype(F32), axis=1).reshape(experts, capacity)
    gate_part = jnp.sum(pick.astype(F32) * row_gate[:, :, None], axis=1)
    gate_part = jnp.broadcast_to(gate_part[:, None, :], (experts, 8, local_tokens))
    mixed, grad_total, gate_all = reduce_all(pipes, experts, mixed_part, grad_part, gate_part)
    named = routes[:, :, None] == jnp.arange(experts)[None, None, :]
    grad_gates = jnp.sum(jnp.where(named, gate_all[:, 0, :].T[:, None, :], 0.0), axis=2)
    return (mixed, grad_total, grad_gates, grad_gate_w[None], grad_up_w[None], grad_down_w[None])


def solution(mesh):
    rows = P("expert", None)
    weights = P("expert", "pipe", None)
    return jax.shard_map(
        body,
        mesh=mesh,
        in_specs=(rows,) * 5 + (weights,) * 3,
        out_specs=(P("expert", "pipe"), P("expert", "pipe"), rows) + (weights,) * 3,
        check_vma=False,
    )
```

time: 288 us -> 174 us (0.60)
  Pallas kernels: 0 us -> 126 us
  waiting for transfers between devices: 85.8 us -> 0 us
  blocking collectives: 74.8 us -> 0 us
  local copies, waits for them, and re-layouts: 43.1 us -> 6.62 us
  between operations: 14 us -> 0.81 us
  starting transfers between devices: 13 us -> 0 us
  other arithmetic: 13.5 us -> 3.58 us
  matrix products: 41.3 us -> 36 us
    pallas_call x0 -> x2, Pallas kernels: none -> 126 us  [the longest x1 64.2 us: reduce_all(): pl.pallas_call(functools.partial(reduce_kernel, pipes, experts), out_shap...]
    all_to_all x3 -> x0, blocking collectives: 70.5 us -> none  [the longest x1 32 us: body(): lax.all_to_all(fill_rows(x_share), 'expert', split_axis=0, concat_axis=0,...]
    all_to_all x2 -> x0, waiting for transfers between devices: 69.8 us -> none  [the longest x1 38.9 us: body(): lax.all_to_all(partial_out.reshape(sources, capacity, width), 'expert', s...]
    gather x4 -> x0, local copies, waits for them, and re-layouts: 19.2 us -> none  [the longest x2 10.1 us: pick_rows(): jnp.take(flat_back, flat_slot, axis=0)]
    all_to_all x2 -> x0, starting transfers between devices: 12.6 us -> none  [the longest x1 6.52 us: body(): lax.all_to_all(partial_out.reshape(sources, capacity, width), 'expert', s...]
    scatter x2 -> x0, local copies, waits for them, and re-layouts: 12 us -> none  [the longest x1 8.61 us: body(): gate_slot = jnp.zeros((slot_total,), jnp.bfloat16).at[flat_slot].set(gate...]
    all_gather x2 -> x0, waiting for transfers between devices: 10.4 us -> none  [the longest x1 10.4 us: body(): lax.all_gather(part_dy, 'pipe', axis=2, tiled=True)]
    reshape x5 -> x0, local copies, waits for them, and re-layouts: 6.22 us -> none  [the longest x2 4.96 us: pick_rows(): jnp.take(flat_back, flat_slot, axis=0)]
  transfers between devices with their start and end apart: 6 -> 0, of which waited for: 4 -> 0; matrix products, arithmetic and copies ran while one was open for 20% -> 0% of each run, Pallas kernels for 0% -> 0%
where the time goes in v1:
time: 174 us; the launch traced here: 173 us
  Pallas kernels  126 us (72%)
  matrix products  36 us (21%)
  local copies, waits for them, and re-layouts  6.62 us (4%)
  other arithmetic  3.58 us (2%)
    pallas_call x1, Pallas kernels, reduce_all(): pl.pallas_call(functools.partial(reduce_kernel, pipes, experts), out_shap...  64.2 us
    pallas_call x1, Pallas kernels, gather_all(): pl.pallas_call(functools.partial(gather_kernel, pipes, experts), out_shap...  61.4 us
    dot_general x1, matrix products, body(): grad_up_w = dot(d_up, x, over_rows).astype(BF16)  4.93 us
    dot_general x3, matrix products, select(): lax.dot_general(matrix, source, by_token, preferred_element_type=F32)  4.48 us
    unnamed x24, local copies, waits for them, and re-layouts  4.19 us
    dot_general x1, matrix products, body(): d_act = dot(d_out, down_w, contract)  4.09 us

profile of v1, /device:TPU:9, one launch (start us, length us, event | category | flops | bytes accessed | tf_op | source)
XLA Modules:
  0.0 172.6 jit_solution(1358734870433189182)
XLA Ops:
  0.6 0.0 copy-start
  0.7 0.8 add_convert_fusion.1
  1.5 0.7 convert_element_type.74
  2.2 0.6 maximum_bitcast_fusion.meta
  2.8 61.4 %gather_rows.1 = (bf16[16,128,1024]{2,1,0:T(8,128)(2,1)}, bf16[16,128,1024]{2,1,0:T(8,128)(2,1)}, f32[16,16,128]{2,1,0:T(8,128)}) custom-call(bf16[128,1024]{1,0:T(8,128)(2,1)} %x.1, bf16[128,1024]{1,0:T(8,128)(2,1)} %dy.1, f32[16,128]{1,0:T(8,128)} %maximum_bitcast_fusion.meta), custom_call_target="tpu_custom_call" | custom-call | tf_op jit(solution)/shard_map/gather_rows/pallas_call | solution.py:135
  64.2 0.9 fusion.19
  65.1 0.6 fusion.1
  65.7 3.0 %convolution_convert_fusion.4 = bf16[16,64,1024]{2,1,0:T(8,128)(2,1)S(1)} fusion(bf16[16,64,128]{2,1,0:T(8,128)(2,1)S(1)} %get-tuple-element.19, bf16[16,128,1024]{2,1,0:T(8,128)(2,1)} %get-tuple-element.13), kind=kOutput, calls=%fused_computation.16 | convolution fusion | flops 269484032 | bytes 6553600 | tf_op jit(solution)/shard_map/dot_general | solution.py:337
  68.8 0.4 copy-done.1
  69.1 0.7 convolution_convert_fusion.3
  69.9 0.0 copy-start.7
  69.9 0.7 convolution_convert_fusion.2
  70.6 0.6 copy-done.7
  71.2 1.7 fusion.11
  73.0 1.7 fusion.15
  74.7 4.1 %multiply_convert_fusion = (bf16[1024,704]{0,1:T(8,128)(2,1)}, bf16[1024,704]{0,1:T(8,128)(2,1)}, bf16[1024,704]{0,1:T(8,128)(2,1)S(1)}) fusion(f32[1024,704]{0,1:T(8,128)S(1)} %fusion.15, f32[1024,704]{0,1:T(8,128)S(1)} %fusion.11, bf16[1024,1024]{1,0:T(8,128)(2,1)S(1)} %bitcast.68, bf16[1,704,1024]{2,1,0:T(8,128)(2,1)S(1)} %copy-done), kind=kOutput, calls=%fused_computation.7 | convolution fusion | flops 1487208448 | bytes 13631488 | tf_op jit(solution)/shard_map/dot_general | solution.py:354
  78.8 2.8 %fusion.6 = bf16[1,704,1024]{2,1,0:T(8,128)(2,1)} fusion(bf16[1024,704]{0,1:T(8,128)(2,1)S(1)} %get-tuple-element.22, bf16[1024,1024]{1,0:T(8,128)(2,1)S(1)} %bitcast.69), kind=kOutput, calls=%fused_computation.23 | convolution fusion | flops 1477115904 | bytes 4980736 | tf_op jit(solution)/shard_map/dot_general | solution.py:360
  81.5 3.4 %fusion = (f32[1024]{0:T(1024)S(1)}, bf16[1024,1024]{1,0:T(8,128)(2,1)}) fusion(bf16[16,64,1024]{2,1,0:T(8,128)(2,1)S(1)} %convolution_convert_fusion.2, bf16[1024,704]{0,1:T(8,128)(2,1)S(1)} %get-tuple-element.22, bf16[1,704,1024]{2,1,0:T(8,128)(2,1)S(1)} %copy-done), kind=kOutput, calls=%fused_computation.1 | convolution fusion | flops 1481636864 | bytes 7081984 | tf_op jit(solution)/shard_map/dot_general | solution.py:353
  84.9 0.1 mul.54
  85.0 0.2 multiply_reduce_fusion
  85.2 0.6 broadcast_in_dim.51.gate
  85.8 4.9 %fusion.5 = bf16[1,704,1024]{2,1,0:T(8,128)(2,1)} fusion(bf16[1024,704]{0,1:T(8,128)(2,1)} %get-tuple-element.20, bf16[1024,1024]{1,0:T(8,128)(2,1)} %bitcast.65), kind=kOutput, calls=%fused_computation.22 | convolution fusion | flops 1477115904 | bytes 4980736 | tf_op jit(solution)/shard_map/dot_general | solution.py:359
  90.8 2.8 %fusion.4 = bf16[1,704,1024]{2,1,0:T(8,128)(2,1)} fusion(bf16[1024,704]{0,1:T(8,128)(2,1)S(1)} %copy-done.9, bf16[1024,1024]{1,0:T(8,128)(2,1)S(1)} %bitcast.66), kind=kOutput, calls=%fused_computation.21 | convolution fusion | flops 1477115904 | bytes 4980736 | tf_op jit(solution)/shard_map/dot_general | solution.py:358
  93.6 3.2 %convolution_convert_fusion.1 = bf16[16,128,1024]{2,1,0:T(8,128)(2,1)} fusion(bf16[16,64,1024]{2,1,0:T(8,128)(2,1)S(1)} %bitcast.67, bf16[16,64,128]{2,1,0:T(8,128)(2,1)S(1)} %get-tuple-element.18), kind=kOutput, calls=%fused_computation.13 | convolution fusion | flops 270532608 | bytes 6553600 | tf_op jit(solution)/shard_map/dot_general | solution.py:364
  96.8 1.8 %fusion.13 = f32[1024,1024]{1,0:T(8,128)S(1)} fusion(bf16[1024,704]{0,1:T(8,128)(2,1)S(1)} %copy-done.9, bf16[1,704,1024]{2,1,0:T(8,128)(2,1)S(1)} %copy-done.6), kind=kOutput, calls=%fused_computation.30 | convolution fusion | flops 1476395008 | bytes 7077888 | tf_op jit(solution)/shard_map/dot_general | solution.py:357
  98.7 1.9 %add_convert_fusion = bf16[1024,1024]{1,0:T(8,128)(2,1)S(1)} fusion(f32[1024,1024]{1,0:T(8,128)S(1)} %fusion.13, bf16[1024,704]{0,1:T(8,128)(2,1)S(1)} %copy-done.10, bf16[1,704,1024]{2,1,0:T(8,128)(2,1)S(1)} %copy-done.8), kind=kOutput, calls=%fused_computation.2 | convolution fusion | flops 1478492160 | bytes 9175040 | tf_op jit(solution)/shard_map/dot_general | solution.py:357
  100.5 3.3 %convolution_convert_fusion = bf16[16,128,1024]{2,1,0:T(8,128)(2,1)} fusion(bf16[16,64,128]{2,1,0:T(8,128)(2,1)S(1)} %get-tuple-element.19, bf16[16,64,1024]{2,1,0:T(8,128)(2,1)S(1)} %bitcast.70), kind=kOutput, calls=%fused_computation.12 | convolution fusion | flops 270532608 | bytes 6553600 | tf_op jit(solution)/shard_map/dot_general | solution.py:365
  103.8 64.2 %reduce_rows.1 = (bf16[128,512]{1,0:T(8,128)(2,1)}, bf16[128,512]{1,0:T(8,128)(2,1)}, f32[16,8,128]{2,1,0:T(8,128)}) custom-call(bf16[4,2,2,128,1024]{4,3,2,1,0:T(8,128)(2,1)} %bitcast.61, bf16[4,2,2,128,1024]{4,3,2,1,0:T(8,128)(2,1)} %bitcast.62, f32[16,8,128]{2,1,0:T(8,128)} %broadcast_in_dim.51.gate), custom_call_target="tpu_custom_call" | custom-call | tf_op jit(solution)/shard_map/reduce_rows/pallas_call | solution.py:287
  168.0 0.8 slice.11
  168.8 0.6 select_reduce_fusion
  169.4 1.6 copy.18
  171.0 1.6 copy.19
  (20 shorter events, 0.0 us)
Async XLA Ops:
  0.6 74.0 %copy-start = (bf16[1,704,1024]{2,1,0:T(8,128)(2,1)S(1)}, bf16[1,704,1024]{2,1,0:T(8,128)(2,1)}, u32[]{:S(2)}) copy-start(bf16[1,704,1024]{2,1,0:T(8,128)(2,1)} %param.15) | copy-start | bytes 4325380
  65.7 3.5 %copy-start.1 = (bf16[16,128,1024]{2,1,0:T(8,128)(2,1)S(1)}, bf16[16,128,1024]{2,1,0:T(8,128)(2,1)}, u32[]{:S(2)}) copy-start(bf16[16,128,1024]{2,1,0:T(8,128)(2,1)} %get-tuple-element.14) | copy-start | bytes 12582916
  68.8 4.2 %copy-start.2 = (bf16[16,64,1024]{2,1,0:T(8,128)(2,1)}, bf16[16,64,1024]{2,1,0:T(8,128)(2,1)S(1)}, u32[]{:S(2)}) copy-start(bf16[16,64,1024]{2,1,0:T(8,128)(2,1)S(1)} %convolution_convert_fusion.4) | copy-start | bytes 6291460
  69.9 1.4 copy-start.7
  71.2 1.7 copy-start.6
  85.8 4.9 %copy-start.3 = (bf16[16,64,1024]{2,1,0:T(8,128)(2,1)S(1)}, bf16[16,64,1024]{2,1,0:T(8,128)(2,1)}, u32[]{:S(2)}) copy-start(bf16[16,64,1024]{2,1,0:T(8,128)(2,1)} %copy-done.2) | copy-start | bytes 6291460
  85.8 4.9 %copy-start.9 = (bf16[1024,704]{0,1:T(8,128)(2,1)S(1)}, bf16[1024,704]{0,1:T(8,128)(2,1)}, u32[]{:S(2)}) copy-start(bf16[1024,704]{0,1:T(8,128)(2,1)} %get-tuple-element.21) | copy-start | bytes 4325380
  90.8 2.8 %copy-start.4 = (bf16[1024,1024]{1,0:T(8,128)(2,1)S(1)}, bf16[1024,1024]{1,0:T(8,128)(2,1)}, u32[]{:S(2)}) copy-start(bf16[1024,1024]{1,0:T(8,128)(2,1)} %get-tuple-element.26) | copy-start | bytes 6291460
  96.8 1.8 %copy-start.8 = (bf16[1,704,1024]{2,1,0:T(8,128)(2,1)S(1)}, bf16[1,704,1024]{2,1,0:T(8,128)(2,1)}, u32[]{:S(2)}) copy-start(bf16[1,704,1024]{2,1,0:T(8,128)(2,1)} %param.14) | copy-start | bytes 4325380
  96.8 1.9 %copy-start.10 = (bf16[1024,704]{0,1:T(8,128)(2,1)S(1)}, bf16[1024,704]{0,1:T(8,128)(2,1)}, u32[]{:S(2)}) copy-start(bf16[1024,704]{0,1:T(8,128)(2,1)} %get-tuple-element.20) | copy-start | bytes 4325380
  103.8 65.0 %copy-start.5 = (s32[128,6]{0,1:T(8,128)S(1)}, s32[128,6]{0,1:T(8,128)}, u32[]{:S(2)}) copy-start(s32[128,6]{0,1:T(8,128)} %param.10) | copy-start | bytes 9220

commit v2 on v1

--- a/solution.py
+++ b/solution.py
@@ -50,7 +50,8 @@
     lanes = 2 * outer - 1
     base = {"z": 0, "y": outer - 1, "own": 2 * outer - 1, "c": 2 * outer, "x": 2 * outer + lanes}
     base["cx"] = base["x"] + lanes
-    return outer, lanes, base, base["cx"] + lanes
+    base["down"] = base["cx"] + lanes
+    return outer, lanes, base, base["down"] + outer - 1
 
 
 def gather_kernel(pipes, experts, x, dy, meta, xg, dyg, mg, send, recv, msend, mrecv, local):
@@ -81,6 +82,14 @@
     for d in range(1, experts):
         go(meta, mg.at[me], msend.at[d - 1], mrecv.at[d - 1], peer(expert=(me + d) % experts))
     arrays = ((x, xg), (dy, dyg))
+    inner = jnp.minimum(z, outer - 1 - z)
+    below_more = z > outer - 1 - z
+
+    def nearest(n):
+        paired = n < 2 * inner
+        below = jnp.where(paired, n % 2 == 0, below_more)
+        far = jnp.where(paired, n // 2 + 1, n - inner + 1)
+        return below, jnp.where(below, far, outer - far)
 
     def sems(a, i):
         return send.at[a * count + i], recv.at[a * count + i]
@@ -88,30 +97,66 @@
     def arrived(ref, a, i):
         remote(ref, ref, *sems(a, i), cpeer).wait_recv()
 
-    for a, (s, g) in enumerate(arrays):
-        for d in range(1, outer):
-            go(s.at[:, wide], g.at[me, :, wide], *sems(a, base["z"] + d - 1),
-               peer(expert=join((z + d) % outer, y, c)))
+    later = []
+
+    def chain(src, block, a, up, down, slot_up, slot_down, dev_up, dev_down):
+        g = arrays[a][1]
+        for way, go_there, slot, dev in (("z", up, slot_up, dev_up),
+                                         ("down", down, slot_down, dev_down)):
+            copy = remote(src, g.at[block, :, wide], send.at[a * count + base[way] + slot - 1],
+                          recv.at[a * count + base["z"] + slot - 1], dev)
+            pl.when(go_there)(copy.start)
+            later.append((go_there, copy))
+
+    above = peer(expert=join(jnp.minimum(z + 1, outer - 1), y, c))
+    under = peer(expert=join(jnp.maximum(z - 1, 0), y, c))
+
+    def start(a):
+        s, g = arrays[a]
+        chain(s.at[:, wide], me, a, z < outer - 1, z > 0, 1, outer - 1, above, under)
         go(s.at[:, wide], g.at[me, :, wide], *sems(a, base["y"]), ypeer)
         go(s, g.at[me], *sems(a, base["own"]), cpeer)
-    for a, (s, g) in enumerate(arrays):
-        for d in range(1, outer):
-            b = join((z + outer - d) % outer, y, c)
-            arrived(g.at[b, :, wide], a, base["z"] + d - 1)
-            go(g.at[b, :, wide], g.at[b, :, wide], *sems(a, base["y"] + d), ypeer)
-            go(g.at[b, :, give], g.at[b, :, give], *sems(a, base["x"] + d - 1), xpeer)
-            go(g.at[b, :, wide], g.at[b, :, wide], *sems(a, base["c"] + d - 1), cpeer)
-        for d in range(outer):
-            b = join((z + outer - d) % outer, 1 - y, c)
-            arrived(g.at[b, :, wide], a, base["y"] + d)
-            go(g.at[b, :, give], g.at[b, :, give], *sems(a, base["x"] + outer - 1 + d), xpeer)
-            go(g.at[b, :, wide], g.at[b, :, wide], *sems(a, base["c"] + outer - 1 + d), cpeer)
-    for a, (s, g) in enumerate(arrays):
-        for i in range(lanes):
-            b = (join((z + outer - i - 1) % outer, y, c) if i < outer - 1
-                 else join((z + outer - (i - outer + 1)) % outer, 1 - y, c))
-            arrived(g.at[b, :, take], a, base["x"] + i)
-            go(g.at[b, :, take], g.at[b, :, take], *sems(a, base["cx"] + i), cpeer)
+
+    def z_event(a, n):
+        g = arrays[a][1]
+        below, d = nearest(n)
+        b = join((z + outer - d) % outer, y, c)
+        ref = g.at[b, :, wide]
+        arrived(ref, a, base["z"] + d - 1)
+        chain(ref, b, a, below & (z < outer - 1), jnp.logical_not(below) & (z > 0),
+              jnp.minimum(d + 1, outer - 1), jnp.maximum(d - 1, 1), above, under)
+        go(ref, ref, *sems(a, base["y"] + d), ypeer)
+        go(g.at[b, :, give], g.at[b, :, give], *sems(a, base["x"] + d - 1), xpeer)
+        go(ref, ref, *sems(a, base["c"] + d - 1), cpeer)
+
+    def y_event(a, n):
+        g = arrays[a][1]
+        d = 0 if n < 0 else nearest(n)[1]
+        b = join((z + outer - d) % outer, 1 - y, c)
+        ref = g.at[b, :, wide]
+        arrived(ref, a, base["y"] + d)
+        go(g.at[b, :, give], g.at[b, :, give], *sems(a, base["x"] + outer - 1 + d), xpeer)
+        go(ref, ref, *sems(a, base["c"] + outer - 1 + d), cpeer)
+
+    def x_event(a, n, across):
+        g = arrays[a][1]
+        d = 0 if n < 0 else nearest(n)[1]
+        b = join((z + outer - d) % outer, 1 - y if across else y, c)
+        i = outer - 1 + d if across else d - 1
+        arrived(g.at[b, :, take], a, base["x"] + i)
+        go(g.at[b, :, take], g.at[b, :, take], *sems(a, base["cx"] + i), cpeer)
+
+    steps = []
+    for a in range(2):
+        at = 2 * outer * a
+        steps += [(at - 1, start, (a,))] if a else []
+        steps += [(at + 2 * n, z_event, (a, n)) for n in range(outer - 1)]
+        steps += [(at + 2 * n + 3, y_event, (a, n)) for n in range(-1, outer - 1)]
+        steps += [(at + 2 * n + 6, x_event, (a, n, False)) for n in range(outer - 1)]
+        steps += [(at + 2 * n + 8, x_event, (a, n, True)) for n in range(-1, outer - 1)]
+    start(0)
+    for _, run, args in sorted(steps, key=lambda step: step[0]):
+        run(*args)
     for a, (s, g) in enumerate(arrays):
         arrived(g.at[join(z, y, 1 - c)], a, base["own"])
         for i in range(lanes):
@@ -119,6 +164,8 @@
                  else join((z + outer - (i - outer + 1)) % outer, 1 - y, 1 - c))
             arrived(g.at[b, :, wide], a, base["c"] + i)
             arrived(g.at[b, :, take], a, base["cx"] + i)
+    for go_there, copy in later:
+        pl.when(go_there)(copy.wait_send)
     for d in range(1, experts):
         b = (me + experts - d) % experts
         remote(mg.at[b], mg.at[b], msend.at[d - 1], mrecv.at[d - 1], cpeer).wait_recv()
@@ -153,13 +200,17 @@
     outer = experts // (INNER * INNER)
     groups = min(outer, 4)
     chunks = 2 * groups
-    base = {"c": 0, "x": chunks, "y": chunks * pipes}
-    base["z"] = base["y"] + groups
-    return outer, groups, base, base["z"] + outer - 1
+    sizes = (("c", chunks), ("xa", chunks * (pipes - 1)), ("ya", groups), ("yb", groups),
+             ("xb", groups * (pipes - 1)), ("za", outer - 1), ("zb", outer - 1))
+    base, total = {}, 0
+    for name, size in sizes:
+        base[name] = total
+        total += size
+    return outer, groups, base, total
 
 
 def reduce_kernel(pipes, experts, pm, pg, gate, om, og, ogate,
-                  stay, come, xin, half, yin, line, zin, gin, gx,
+                  stay, come, xain, half, yain, ybin, mid, xbin, line, zin, gin, gx,
                   send, recv, gsend, grecv, gxs, gxr, local):
     me, z, y, c = place(experts)
     p = lax.axis_index("pipe")
@@ -167,6 +218,8 @@
     size = outer // groups
     chunks = 2 * groups
     share = om.shape[1]
+    top = om.shape[0] // 2
+    rows_a, rows_b = pl.ds(0, top), pl.ds(top, top)
     cpeer = peer(expert=join(z, y, 1 - c))
     ypeer = peer(expert=join(z, 1 - y, c))
     mine = pl.ds(pl.multiple_of(p * share, 128), share)
@@ -176,9 +229,6 @@
     def where(k):
         g = (z // size + 1 + k % groups) % groups
         return (y + 1 + k // groups) % 2, pl.ds(g * size, size)
-
-    def where_peer(k):
-        return where(k)
 
     loads = []
     for a in range(2):
@@ -212,67 +262,103 @@
             yy, zz = where(k)
             go(parts[a].at[zz, yy, 1 - c], come.at[a, yy, zz], *sems(a, base["c"] + k), cpeer)
 
+    def plus(left, right):
+        return (left.astype(F32) + right.astype(F32)).astype(BF16)
+
     def core_step(a, k):
         yy, zz = where(k)
         loads[a * chunks + k].wait()
         arrived(come.at[a, yy, zz], a, base["c"] + k)
-        stay[a, yy, zz] = (stay[a, yy, zz].astype(F32) + come[a, yy, zz].astype(F32)).astype(BF16)
+        stay[a, yy, zz] = plus(stay[a, yy, zz], come[a, yy, zz])
+        if k < groups:
+            go(stay.at[a, yy, zz, rows_b], ybin.at[a, zz], *sems(a, base["yb"] + k), ypeer)
         for j in range(1, pipes):
             to = (p + j) % pipes
             cols = pl.ds(pl.multiple_of(to * share, 128), share)
-            go(stay.at[a, yy, zz, :, cols], xin.at[a, j - 1, yy, zz],
-               *sems(a, base["x"] + (j - 1) * chunks + k), peer(pipe=to))
-
-    def x_step(a, k):
+            go(stay.at[a, yy, zz, rows_a, cols], xain.at[a, j - 1, yy, zz],
+               *sems(a, base["xa"] + (j - 1) * chunks + k), peer(pipe=to))
+
+    def xa_step(a, k):
         yy, zz = where(k)
-        total = stay[a, yy, zz, :, mine].astype(F32)
+        total = stay[a, yy, zz, rows_a, mine].astype(F32)
         for j in range(1, pipes):
-            arrived(xin.at[a, j - 1, yy, zz], a, base["x"] + (j - 1) * chunks + k)
-            total = total + xin[a, j - 1, yy, zz].astype(F32)
+            arrived(xain.at[a, j - 1, yy, zz], a, base["xa"] + (j - 1) * chunks + k)
+            total = total + xain[a, j - 1, yy, zz].astype(F32)
         half[a, yy, zz] = total.astype(BF16)
         if k < groups:
-            go(half.at[a, yy, zz], yin.at[a, zz], *sems(a, base["y"] + k), ypeer)
-
-    def y_step(a, k):
+            go(half.at[a, yy, zz], yain.at[a, zz], *sems(a, base["ya"] + k), ypeer)
+
+    def yb_step(a, k):
         yy, zz = where(groups + k)
-        arrived(yin.at[a, zz], a, base["y"] + k)
-        line[a, zz] = (half[a, yy, zz].astype(F32) + yin[a, zz].astype(F32)).astype(BF16)
-        if size == 1 and k < groups - 1:
-            z_send(a, k + 1)
-
-    def z_send(a, d):
+        arrived(ybin.at[a, zz], a, base["yb"] + k)
+        mid[a, zz] = plus(stay[a, yy, zz, rows_b], ybin[a, zz])
+        for j in range(1, pipes):
+            to = (p + j) % pipes
+            cols = pl.ds(pl.multiple_of(to * share, 128), share)
+            go(mid.at[a, zz, :, cols], xbin.at[a, j - 1, zz],
+               *sems(a, base["xb"] + (j - 1) * groups + k), peer(pipe=to))
+
+    def z_send(a, h, d):
         to = (z + d) % outer
-        go(line.at[a, to], zin.at[a, d - 1], *sems(a, base["z"] + d - 1),
+        go(line.at[a, h, to], zin.at[a, h, d - 1], *sems(a, base["zb" if h else "za"] + d - 1),
            peer(expert=join(to, y, c)))
+
+    def line_done(a, h, k):
+        if size == 1:
+            if k < groups - 1:
+                z_send(a, h, k + 1)
+        elif k == groups - 1:
+            for d in range(1, outer):
+                z_send(a, h, d)
+
+    def ya_step(a, k):
+        yy, zz = where(groups + k)
+        arrived(yain.at[a, zz], a, base["ya"] + k)
+        line[a, 0, zz] = plus(half[a, yy, zz], yain[a, zz])
+        line_done(a, 0, k)
+
+    def xb_step(a, k):
+        _, zz = where(k)
+        total = mid[a, zz, :, mine].astype(F32)
+        for j in range(1, pipes):
+            arrived(xbin.at[a, j - 1, zz], a, base["xb"] + (j - 1) * groups + k)
+            total = total + xbin[a, j - 1, zz].astype(F32)
+        line[a, 1, zz] = total.astype(BF16)
+        line_done(a, 1, k)
+
+    def gate_step():
+        for d in range(1, experts):
+            b = (me + experts - d) % experts
+            remote(gin.at[b], gin.at[b], gsend.at[d - 1], grecv.at[d - 1], cpeer).wait_recv()
+        keep.wait()
+        for j in range(1, pipes):
+            go(gin, gx.at[j - 1], gxs.at[j - 1], gxr.at[j - 1], peer(pipe=(p + j) % pipes))
 
     for a in range(2):
         for k in range(chunks):
             core_step(a, k)
-    for d in range(1, experts):
-        b = (me + experts - d) % experts
-        remote(gin.at[b], gin.at[b], gsend.at[d - 1], grecv.at[d - 1], cpeer).wait_recv()
-    keep.wait()
-    for j in range(1, pipes):
-        go(gin, gx.at[j - 1], gxs.at[j - 1], gxr.at[j - 1], peer(pipe=(p + j) % pipes))
-    for a in range(2):
-        for k in range(chunks):
-            x_step(a, k)
+    for a in range(2):
         for k in range(groups):
-            y_step(a, k)
-        if size > 1:
-            for d in range(1, outer):
-                z_send(a, d)
+            xa_step(a, k)
+            yb_step(a, k)
+        for k in range(groups):
+            xa_step(a, groups + k)
+            ya_step(a, k)
+            xb_step(a, k)
+        if a == 0:
+            gate_step()
     whole = gin[...]
     for j in range(1, pipes):
         remote(gin, gx.at[j - 1], gxs.at[j - 1], gxr.at[j - 1], cpeer).wait_recv()
         whole = whole + gx[j - 1]
     ogate[...] = whole
     for a in range(2):
-        total = line[a, z].astype(F32)
-        for d in range(1, outer):
-            arrived(zin.at[a, d - 1], a, base["z"] + d - 1)
-            total = total + zin[a, d - 1].astype(F32)
-        outs[a][...] = total.astype(BF16)
+        for h in range(2):
+            total = line[a, h, z].astype(F32)
+            for d in range(1, outer):
+                arrived(zin.at[a, h, d - 1], a, base["zb" if h else "za"] + d - 1)
+                total = total + zin[a, h, d - 1].astype(F32)
+            outs[a][h * top:(h + 1) * top] = total.astype(BF16)
     for copy in sent:
         copy.wait_send()
 
@@ -281,6 +367,7 @@
     outer, groups, base, count = reduce_plan(pipes, experts)
     rows, width = mixed.shape[1:]
     share = width // pipes
+    top = rows // 2
     shape = (outer, INNER, INNER, rows, width)
     hbm = pl.BlockSpec(memory_space=pl.ANY)
     vmem = pl.BlockSpec(memory_space=pltpu.VMEM)
@@ -293,11 +380,14 @@
         scratch_shapes=[
             pltpu.VMEM((2, INNER, outer, rows, width), BF16),
             pltpu.VMEM((2, INNER, outer, rows, width), BF16),
-            pltpu.VMEM((2, pipes - 1, INNER, outer, rows, share), BF16),
-            pltpu.VMEM((2, INNER, outer, rows, share), BF16),
-            pltpu.VMEM((2, outer, rows, share), BF16),
-            pltpu.VMEM((2, outer, rows, share), BF16),
-            pltpu.VMEM((2, outer - 1, rows, share), BF16),
+            pltpu.VMEM((2, pipes - 1, INNER, outer, top, share), BF16),
+            pltpu.VMEM((2, INNER, outer, top, share), BF16),
+            pltpu.VMEM((2, outer, top, share), BF16),
+            pltpu.VMEM((2, outer, top, width), BF16),
+            pltpu.VMEM((2, outer, top, width), BF16),
+            pltpu.VMEM((2, pipes - 1, outer, top, share), BF16),
+            pltpu.VMEM((2, 2, outer, top, share), BF16),
+            pltpu.VMEM((2, 2, outer - 1, top, share), BF16),
             pltpu.VMEM(gate.shape, F32),
             pltpu.VMEM((pipes - 1,) + gate.shape, F32),
             pltpu.SemaphoreType.DMA((2 * count,)),

time: 174 us -> 161 us (0.925)
  Pallas kernels: 126 us -> 114 us
    pallas_call x1, Pallas kernels: 61.4 us -> 51.3 us  [gather_all(): pl.pallas_call(functools.partial(gather_kernel, pipes, experts), out_shap...]
where the time goes in v2:
time: 161 us
  Pallas kernels  114 us (71%)
  matrix products  36 us (22%)
  local copies, waits for them, and re-layouts  6.62 us (4%)
  other arithmetic  3.58 us (2%)
    pallas_call x1, Pallas kernels, reduce_all(): pl.pallas_call(functools.partial(reduce_kernel, pipes, experts), out_shap...  62.6 us
    pallas_call x1, Pallas kernels, gather_all(): pl.pallas_call(functools.partial(gather_kernel, pipes, experts), out_shap...  51.3 us
    dot_general x1, matrix products, body(): grad_up_w = dot(d_up, x, over_rows).astype(BF16)  4.93 us
    dot_general x3, matrix products, select(): lax.dot_general(matrix, source, by_token, preferred_element_type=F32)  4.47 us
    unnamed x24, local copies, waits for them, and re-layouts  4.19 us
    dot_general x1, matrix products, body(): d_act = dot(d_out, down_w, contract)  4.09 us
    dot_general x1, matrix products, body(): partial_out = dot(act, down_w, plain).astype(BF16)  3.4 us
    dot_general x1, matrix products, body(): grad_part = dot(pick, partial_back.reshape(shape), over_slots).astype(BF16)  3.26 us

profile of v2, /device:TPU:9, one launch (start us, length us, event | category | flops | bytes accessed | tf_op | source)
XLA Modules:
  0.0 161.0 jit_solution(3692563226362822631)
XLA Ops:
  0.6 0.0 copy-start
  0.7 0.8 add_convert_fusion.1
  1.5 0.7 convert_element_type.74
  2.2 0.6 maximum_bitcast_fusion.meta
  2.8 51.3 %gather_rows.1 = (bf16[16,128,1024]{2,1,0:T(8,128)(2,1)}, bf16[16,128,1024]{2,1,0:T(8,128)(2,1)}, f32[16,16,128]{2,1,0:T(8,128)}) custom-call(bf16[128,1024]{1,0:T(8,128)(2,1)} %x.1, bf16[128,1024]{1,0:T(8,128)(2,1)} %dy.1, f32[16,128]{1,0:T(8,128)} %maximum_bitcast_fusion.meta), custom_call_target="tpu_custom_call" | custom-call | tf_op jit(solution)/shard_map/gather_rows/pallas_call | solution.py:182
  54.1 0.9 fusion.19
  55.0 0.6 fusion.1
  55.7 3.0 %convolution_convert_fusion.4 = bf16[16,64,1024]{2,1,0:T(8,128)(2,1)S(1)} fusion(bf16[16,64,128]{2,1,0:T(8,128)(2,1)S(1)} %get-tuple-element.19, bf16[16,128,1024]{2,1,0:T(8,128)(2,1)} %get-tuple-element.13), kind=kOutput, calls=%fused_computation.16 | convolution fusion | flops 269484032 | bytes 6553600 | tf_op jit(solution)/shard_map/dot_general | solution.py:427
  58.7 0.4 copy-done.1
  59.1 0.7 convolution_convert_fusion.3
  59.8 0.0 copy-start.7
  59.8 0.7 convolution_convert_fusion.2
  60.6 0.6 copy-done.7
  61.2 1.7 %fusion.11 = f32[1024,704]{0,1:T(8,128)S(1)} fusion(bf16[1024,1024]{1,0:T(8,128)(2,1)S(1)} %bitcast.63, bf16[1,704,1024]{2,1,0:T(8,128)(2,1)S(1)} %copy-done.7), kind=kOutput, calls=%fused_computation.28 | convolution fusion | flops 1476395008 | bytes 6422528 | tf_op jit(solution)/shard_map/dot_general | solution.py:439
  62.9 1.7 %fusion.15 = f32[1024,704]{0,1:T(8,128)S(1)} fusion(bf16[1024,1024]{1,0:T(8,128)(2,1)S(1)} %bitcast.64, bf16[1,704,1024]{2,1,0:T(8,128)(2,1)S(1)} %copy-done.6), kind=kOutput, calls=%fused_computation.32 | convolution fusion | flops 1476395008 | bytes 6422528 | tf_op jit(solution)/shard_map/dot_general | solution.py:438
  64.6 4.1 %multiply_convert_fusion = (bf16[1024,704]{0,1:T(8,128)(2,1)}, bf16[1024,704]{0,1:T(8,128)(2,1)}, bf16[1024,704]{0,1:T(8,128)(2,1)S(1)}) fusion(f32[1024,704]{0,1:T(8,128)S(1)} %fusion.15, f32[1024,704]{0,1:T(8,128)S(1)} %fusion.11, bf16[1024,1024]{1,0:T(8,128)(2,1)S(1)} %bitcast.68, bf16[1,704,1024]{2,1,0:T(8,128)(2,1)S(1)} %copy-done), kind=kOutput, calls=%fused_computation.7 | convolution fusion | flops 1487208448 | bytes 13631488 | tf_op jit(solution)/shard_map/dot_general | solution.py:444
  68.7 2.8 %fusion.6 = bf16[1,704,1024]{2,1,0:T(8,128)(2,1)} fusion(bf16[1024,704]{0,1:T(8,128)(2,1)S(1)} %get-tuple-element.22, bf16[1024,1024]{1,0:T(8,128)(2,1)S(1)} %bitcast.69), kind=kOutput, calls=%fused_computation.23 | convolution fusion | flops 1477115904 | bytes 4980736 | tf_op jit(solution)/shard_map/dot_general | solution.py:450
  71.5 3.4 %fusion = (f32[1024]{0:T(1024)S(1)}, bf16[1024,1024]{1,0:T(8,128)(2,1)}) fusion(bf16[16,64,1024]{2,1,0:T(8,128)(2,1)S(1)} %convolution_convert_fusion.2, bf16[1024,704]{0,1:T(8,128)(2,1)S(1)} %get-tuple-element.22, bf16[1,704,1024]{2,1,0:T(8,128)(2,1)S(1)} %copy-done), kind=kOutput, calls=%fused_computation.1 | convolution fusion | flops 1481636864 | bytes 7081984 | tf_op jit(solution)/shard_map/dot_general | solution.py:443
  74.9 0.1 mul.54
  75.0 0.2 multiply_reduce_fusion
  75.2 0.6 broadcast_in_dim.51.gate
  75.8 4.9 %fusion.5 = bf16[1,704,1024]{2,1,0:T(8,128)(2,1)} fusion(bf16[1024,704]{0,1:T(8,128)(2,1)} %get-tuple-element.20, bf16[1024,1024]{1,0:T(8,128)(2,1)} %bitcast.65), kind=kOutput, calls=%fused_computation.22 | convolution fusion | flops 1477115904 | bytes 4980736 | tf_op jit(solution)/shard_map/dot_general | solution.py:449
  80.8 2.8 %fusion.4 = bf16[1,704,1024]{2,1,0:T(8,128)(2,1)} fusion(bf16[1024,704]{0,1:T(8,128)(2,1)S(1)} %copy-done.9, bf16[1024,1024]{1,0:T(8,128)(2,1)S(1)} %bitcast.66), kind=kOutput, calls=%fused_computation.21 | convolution fusion | flops 1477115904 | bytes 4980736 | tf_op jit(solution)/shard_map/dot_general | solution.py:448
  83.5 3.2 %convolution_convert_fusion.1 = bf16[16,128,1024]{2,1,0:T(8,128)(2,1)} fusion(bf16[16,64,1024]{2,1,0:T(8,128)(2,1)S(1)} %bitcast.67, bf16[16,64,128]{2,1,0:T(8,128)(2,1)S(1)} %get-tuple-element.18), kind=kOutput, calls=%fused_computation.13 | convolution fusion | flops 270532608 | bytes 6553600 | tf_op jit(solution)/shard_map/dot_general | solution.py:454
  86.8 1.8 %fusion.13 = f32[1024,1024]{1,0:T(8,128)S(1)} fusion(bf16[1024,704]{0,1:T(8,128)(2,1)S(1)} %copy-done.9, bf16[1,704,1024]{2,1,0:T(8,128)(2,1)S(1)} %copy-done.6), kind=kOutput, calls=%fused_computation.30 | convolution fusion | flops 1476395008 | bytes 7077888 | tf_op jit(solution)/shard_map/dot_general | solution.py:447
  88.6 1.9 %add_convert_fusion = bf16[1024,1024]{1,0:T(8,128)(2,1)S(1)} fusion(f32[1024,1024]{1,0:T(8,128)S(1)} %fusion.13, bf16[1024,704]{0,1:T(8,128)(2,1)S(1)} %copy-done.10, bf16[1,704,1024]{2,1,0:T(8,128)(2,1)S(1)} %copy-done.8), kind=kOutput, calls=%fused_computation.2 | convolution fusion | flops 1478492160 | bytes 9175040 | tf_op jit(solution)/shard_map/dot_general | solution.py:447
  90.5 3.3 %convolution_convert_fusion = bf16[16,128,1024]{2,1,0:T(8,128)(2,1)} fusion(bf16[16,64,128]{2,1,0:T(8,128)(2,1)S(1)} %get-tuple-element.19, bf16[16,64,1024]{2,1,0:T(8,128)(2,1)S(1)} %bitcast.70), kind=kOutput, calls=%fused_computation.12 | convolution fusion | flops 270532608 | bytes 6553600 | tf_op jit(solution)/shard_map/dot_general | solution.py:455
  93.8 62.6 %reduce_rows.1 = (bf16[128,512]{1,0:T(8,128)(2,1)}, bf16[128,512]{1,0:T(8,128)(2,1)}, f32[16,8,128]{2,1,0:T(8,128)}) custom-call(bf16[4,2,2,128,1024]{4,3,2,1,0:T(8,128)(2,1)} %bitcast.61, bf16[4,2,2,128,1024]{4,3,2,1,0:T(8,128)(2,1)} %bitcast.62, f32[16,8,128]{2,1,0:T(8,128)} %broadcast_in_dim.51.gate), custom_call_target="tpu_custom_call" | custom-call | tf_op jit(solution)/shard_map/reduce_rows/pallas_call | solution.py:374
  156.4 0.8 slice.11
  157.3 0.6 select_reduce_fusion
  157.9 1.6 copy.18
  159.4 1.6 copy.19
  (20 shorter events, 0.0 us)
Async XLA Ops:
  0.6 64.0 %copy-start = (bf16[1,704,1024]{2,1,0:T(8,128)(2,1)S(1)}, bf16[1,704,1024]{2,1,0:T(8,128)(2,1)}, u32[]{:S(2)}) copy-start(bf16[1,704,1024]{2,1,0:T(8,128)(2,1)} %param.15) | copy-start | bytes 4325380
  55.7 3.5 %copy-start.1 = (bf16[16,128,1024]{2,1,0:T(8,128)(2,1)S(1)}, bf16[16,128,1024]{2,1,0:T(8,128)(2,1)}, u32[]{:S(2)}) copy-start(bf16[16,128,1024]{2,1,0:T(8,128)(2,1)} %get-tuple-element.14) | copy-start | bytes 12582916
  58.7 4.2 %copy-start.2 = (bf16[16,64,1024]{2,1,0:T(8,128)(2,1)}, bf16[16,64,1024]{2,1,0:T(8,128)(2,1)S(1)}, u32[]{:S(2)}) copy-start(bf16[16,64,1024]{2,1,0:T(8,128)(2,1)S(1)} %convolution_convert_fusion.4) | copy-start | bytes 6291460
  59.8 1.4 copy-start.7
  61.2 1.7 %copy-start.6 = (bf16[1,704,1024]{2,1,0:T(8,128)(2,1)S(1)}, bf16[1,704,1024]{2,1,0:T(8,128)(2,1)}, u32[]{:S(2)}) copy-start(bf16[1,704,1024]{2,1,0:T(8,128)(2,1)} %param.13) | copy-start | bytes 4325380
  75.8 4.9 %copy-start.3 = (bf16[16,64,1024]{2,1,0:T(8,128)(2,1)S(1)}, bf16[16,64,1024]{2,1,0:T(8,128)(2,1)}, u32[]{:S(2)}) copy-start(bf16[16,64,1024]{2,1,0:T(8,128)(2,1)} %copy-done.2) | copy-start | bytes 6291460
  75.8 4.9 %copy-start.9 = (bf16[1024,704]{0,1:T(8,128)(2,1)S(1)}, bf16[1024,704]{0,1:T(8,128)(2,1)}, u32[]{:S(2)}) copy-start(bf16[1024,704]{0,1:T(8,128)(2,1)} %get-tuple-element.21) | copy-start | bytes 4325380
  80.8 2.8 %copy-start.4 = (bf16[1024,1024]{1,0:T(8,128)(2,1)S(1)}, bf16[1024,1024]{1,0:T(8,128)(2,1)}, u32[]{:S(2)}) copy-start(bf16[1024,1024]{1,0:T(8,128)(2,1)} %get-tuple-element.26) | copy-start | bytes 6291460
  86.8 1.8 %copy-start.8 = (bf16[1,704,1024]{2,1,0:T(8,128)(2,1)S(1)}, bf16[1,704,1024]{2,1,0:T(8,128)(2,1)}, u32[]{:S(2)}) copy-start(bf16[1,704,1024]{2,1,0:T(8,128)(2,1)} %param.14) | copy-start | bytes 4325380
  86.8 1.9 %copy-start.10 = (bf16[1024,704]{0,1:T(8,128)(2,1)S(1)}, bf16[1024,704]{0,1:T(8,128)(2,1)}, u32[]{:S(2)}) copy-start(bf16[1024,704]{0,1:T(8,128)(2,1)} %get-tuple-element.20) | copy-start | bytes 4325380
  93.8 63.5 %copy-start.5 = (s32[128,6]{0,1:T(8,128)S(1)}, s32[128,6]{0,1:T(8,128)}, u32[]{:S(2)}) copy-start(s32[128,6]{0,1:T(8,128)} %param.10) | copy-start | bytes 9220

commit v3 on v2

--- a/solution.py
+++ b/solution.py
@@ -148,12 +148,12 @@
 
     steps = []
     for a in range(2):
-        at = 2 * outer * a
-        steps += [(at - 1, start, (a,))] if a else []
+        at = (outer + 0.2) * a
+        steps += [(0.5, start, (a,))] if a else []
         steps += [(at + 2 * n, z_event, (a, n)) for n in range(outer - 1)]
         steps += [(at + 2 * n + 3, y_event, (a, n)) for n in range(-1, outer - 1)]
-        steps += [(at + 2 * n + 6, x_event, (a, n, False)) for n in range(outer - 1)]
-        steps += [(at + 2 * n + 8, x_event, (a, n, True)) for n in range(-1, outer - 1)]
+        steps += [(at + 2 * n + 9, x_event, (a, n, False)) for n in range(outer - 1)]
+        steps += [(at + 2 * n + 11, x_event, (a, n, True)) for n in range(-1, outer - 1)]
     start(0)
     for _, run, args in sorted(steps, key=lambda step: step[0]):
         run(*args)
@@ -334,19 +334,26 @@
         for j in range(1, pipes):
             go(gin, gx.at[j - 1], gxs.at[j - 1], gxr.at[j - 1], peer(pipe=(p + j) % pipes))
 
-    for a in range(2):
-        for k in range(chunks):
-            core_step(a, k)
-    for a in range(2):
+    def first_hops(a):
         for k in range(groups):
             xa_step(a, k)
             yb_step(a, k)
+
+    def last_hops(a):
         for k in range(groups):
             xa_step(a, groups + k)
             ya_step(a, k)
             xb_step(a, k)
-        if a == 0:
-            gate_step()
+
+    for k in range(chunks):
+        core_step(0, k)
+    first_hops(0)
+    for k in range(chunks):
+        core_step(1, k)
+    last_hops(0)
+    gate_step()
+    first_hops(1)
+    last_hops(1)
     whole = gin[...]
     for j in range(1, pipes):
         remote(gin, gx.at[j - 1], gxs.at[j - 1], gxr.at[j - 1], cpeer).wait_recv()

time: 161 us -> 152 us (0.944)
  Pallas kernels: 114 us -> 104 us
    pallas_call x1, Pallas kernels: 62.6 us -> 56.3 us  [reduce_all(): pl.pallas_call(functools.partial(reduce_kernel, pipes, experts), out_shap...]
    pallas_call x1, Pallas kernels: 51.3 us -> 47.9 us  [gather_all(): pl.pallas_call(functools.partial(gather_kernel, pipes, experts), out_shap...]
where the time goes in v3:
time: 152 us; the launch traced here: 151 us
  Pallas kernels  104 us (68%)
  matrix products  36 us (24%)
  local copies, waits for them, and re-layouts  6.62 us (4%)
  other arithmetic  3.58 us (2%)
    pallas_call x1, Pallas kernels, reduce_all(): pl.pallas_call(functools.partial(reduce_kernel, pipes, experts), out_shap...  56.3 us
    pallas_call x1, Pallas kernels, gather_all(): pl.pallas_call(functools.partial(gather_kernel, pipes, experts), out_shap...  47.9 us
    dot_general x1, matrix products, body(): grad_up_w = dot(d_up, x, over_rows).astype(BF16)  4.93 us
    dot_general x3, matrix products, select(): lax.dot_general(matrix, source, by_token, preferred_element_type=F32)  4.47 us
    unnamed x24, local copies, waits for them, and re-layouts  4.19 us
    dot_general x1, matrix products, body(): d_act = dot(d_out, down_w, contract)  4.09 us
    dot_general x1, matrix products, body(): partial_out = dot(act, down_w, plain).astype(BF16)  3.4 us
    dot_general x1, matrix products, body(): grad_part = dot(pick, partial_back.reshape(shape), over_slots).astype(BF16)  3.26 us

profile of v3, /device:TPU:9, one launch (start us, length us, event | category | flops | bytes accessed | tf_op | source)
XLA Modules:
  0.0 151.2 jit_solution(5162796250103696278)
XLA Ops:
  0.6 0.0 copy-start
  0.7 0.8 add_convert_fusion.1
  1.5 0.7 convert_element_type.74
  2.2 0.6 maximum_bitcast_fusion.meta
  2.8 47.9 %gather_rows.1 = (bf16[16,128,1024]{2,1,0:T(8,128)(2,1)}, bf16[16,128,1024]{2,1,0:T(8,128)(2,1)}, f32[16,16,128]{2,1,0:T(8,128)}) custom-call(bf16[128,1024]{1,0:T(8,128)(2,1)} %x.1, bf16[128,1024]{1,0:T(8,128)(2,1)} %dy.1, f32[16,128]{1,0:T(8,128)} %maximum_bitcast_fusion.meta), custom_call_target="tpu_custom_call" | custom-call | tf_op jit(solution)/shard_map/gather_rows/pallas_call | solution.py:182
  50.7 0.9 fusion.19
  51.6 0.6 fusion.1
  52.2 3.0 %convolution_convert_fusion.4 = bf16[16,64,1024]{2,1,0:T(8,128)(2,1)S(1)} fusion(bf16[16,64,128]{2,1,0:T(8,128)(2,1)S(1)} %get-tuple-element.19, bf16[16,128,1024]{2,1,0:T(8,128)(2,1)} %get-tuple-element.13), kind=kOutput, calls=%fused_computation.16 | convolution fusion | flops 269484032 | bytes 6553600 | tf_op jit(solution)/shard_map/dot_general | solution.py:434
  55.3 0.4 copy-done.1
  55.7 0.7 convolution_convert_fusion.3
  56.4 0.0 copy-start.7
  56.4 0.7 convolution_convert_fusion.2
  57.1 0.6 copy-done.7
  57.7 1.7 %fusion.11 = f32[1024,704]{0,1:T(8,128)S(1)} fusion(bf16[1024,1024]{1,0:T(8,128)(2,1)S(1)} %bitcast.63, bf16[1,704,1024]{2,1,0:T(8,128)(2,1)S(1)} %copy-done.7), kind=kOutput, calls=%fused_computation.28 | convolution fusion | flops 1476395008 | bytes 6422528 | tf_op jit(solution)/shard_map/dot_general | solution.py:446
  59.5 1.7 %fusion.15 = f32[1024,704]{0,1:T(8,128)S(1)} fusion(bf16[1024,1024]{1,0:T(8,128)(2,1)S(1)} %bitcast.64, bf16[1,704,1024]{2,1,0:T(8,128)(2,1)S(1)} %copy-done.6), kind=kOutput, calls=%fused_computation.32 | convolution fusion | flops 1476395008 | bytes 6422528 | tf_op jit(solution)/shard_map/dot_general | solution.py:445
  61.2 4.1 %multiply_convert_fusion = (bf16[1024,704]{0,1:T(8,128)(2,1)}, bf16[1024,704]{0,1:T(8,128)(2,1)}, bf16[1024,704]{0,1:T(8,128)(2,1)S(1)}) fusion(f32[1024,704]{0,1:T(8,128)S(1)} %fusion.15, f32[1024,704]{0,1:T(8,128)S(1)} %fusion.11, bf16[1024,1024]{1,0:T(8,128)(2,1)S(1)} %bitcast.68, bf16[1,704,1024]{2,1,0:T(8,128)(2,1)S(1)} %copy-done), kind=kOutput, calls=%fused_computation.7 | convolution fusion | flops 1487208448 | bytes 13631488 | tf_op jit(solution)/shard_map/dot_general | solution.py:451
  65.3 2.8 %fusion.6 = bf16[1,704,1024]{2,1,0:T(8,128)(2,1)} fusion(bf16[1024,704]{0,1:T(8,128)(2,1)S(1)} %get-tuple-element.22, bf16[1024,1024]{1,0:T(8,128)(2,1)S(1)} %bitcast.69), kind=kOutput, calls=%fused_computation.23 | convolution fusion | flops 1477115904 | bytes 4980736 | tf_op jit(solution)/shard_map/dot_general | solution.py:457
  68.0 3.4 %fusion = (f32[1024]{0:T(1024)S(1)}, bf16[1024,1024]{1,0:T(8,128)(2,1)}) fusion(bf16[16,64,1024]{2,1,0:T(8,128)(2,1)S(1)} %convolution_convert_fusion.2, bf16[1024,704]{0,1:T(8,128)(2,1)S(1)} %get-tuple-element.22, bf16[1,704,1024]{2,1,0:T(8,128)(2,1)S(1)} %copy-done), kind=kOutput, calls=%fused_computation.1 | convolution fusion | flops 1481636864 | bytes 7081984 | tf_op jit(solution)/shard_map/dot_general | solution.py:450
  71.4 0.1 mul.54
  71.5 0.2 multiply_reduce_fusion
  71.7 0.6 broadcast_in_dim.51.gate
  72.4 4.9 %fusion.5 = bf16[1,704,1024]{2,1,0:T(8,128)(2,1)} fusion(bf16[1024,704]{0,1:T(8,128)(2,1)} %get-tuple-element.20, bf16[1024,1024]{1,0:T(8,128)(2,1)} %bitcast.65), kind=kOutput, calls=%fused_computation.22 | convolution fusion | flops 1477115904 | bytes 4980736 | tf_op jit(solution)/shard_map/dot_general | solution.py:456
  77.3 2.8 %fusion.4 = bf16[1,704,1024]{2,1,0:T(8,128)(2,1)} fusion(bf16[1024,704]{0,1:T(8,128)(2,1)S(1)} %copy-done.9, bf16[1024,1024]{1,0:T(8,128)(2,1)S(1)} %bitcast.66), kind=kOutput, calls=%fused_computation.21 | convolution fusion | flops 1477115904 | bytes 4980736 | tf_op jit(solution)/shard_map/dot_general | solution.py:455
  80.1 3.2 %convolution_convert_fusion.1 = bf16[16,128,1024]{2,1,0:T(8,128)(2,1)} fusion(bf16[16,64,1024]{2,1,0:T(8,128)(2,1)S(1)} %bitcast.67, bf16[16,64,128]{2,1,0:T(8,128)(2,1)S(1)} %get-tuple-element.18), kind=kOutput, calls=%fused_computation.13 | convolution fusion | flops 270532608 | bytes 6553600 | tf_op jit(solution)/shard_map/dot_general | solution.py:461
  83.3 1.8 %fusion.13 = f32[1024,1024]{1,0:T(8,128)S(1)} fusion(bf16[1024,704]{0,1:T(8,128)(2,1)S(1)} %copy-done.9, bf16[1,704,1024]{2,1,0:T(8,128)(2,1)S(1)} %copy-done.6), kind=kOutput, calls=%fused_computation.30 | convolution fusion | flops 1476395008 | bytes 7077888 | tf_op jit(solution)/shard_map/dot_general | solution.py:454
  85.2 1.9 %add_convert_fusion = bf16[1024,1024]{1,0:T(8,128)(2,1)S(1)} fusion(f32[1024,1024]{1,0:T(8,128)S(1)} %fusion.13, bf16[1024,704]{0,1:T(8,128)(2,1)S(1)} %copy-done.10, bf16[1,704,1024]{2,1,0:T(8,128)(2,1)S(1)} %copy-done.8), kind=kOutput, calls=%fused_computation.2 | convolution fusion | flops 1478492160 | bytes 9175040 | tf_op jit(solution)/shard_map/dot_general | solution.py:454
  87.1 3.3 %convolution_convert_fusion = bf16[16,128,1024]{2,1,0:T(8,128)(2,1)} fusion(bf16[16,64,128]{2,1,0:T(8,128)(2,1)S(1)} %get-tuple-element.19, bf16[16,64,1024]{2,1,0:T(8,128)(2,1)S(1)} %bitcast.70), kind=kOutput, calls=%fused_computation.12 | convolution fusion | flops 270532608 | bytes 6553600 | tf_op jit(solution)/shard_map/dot_general | solution.py:462
  90.3 56.3 %reduce_rows.1 = (bf16[128,512]{1,0:T(8,128)(2,1)}, bf16[128,512]{1,0:T(8,128)(2,1)}, f32[16,8,128]{2,1,0:T(8,128)}) custom-call(bf16[4,2,2,128,1024]{4,3,2,1,0:T(8,128)(2,1)} %bitcast.61, bf16[4,2,2,128,1024]{4,3,2,1,0:T(8,128)(2,1)} %bitcast.62, f32[16,8,128]{2,1,0:T(8,128)} %broadcast_in_dim.51.gate), custom_call_target="tpu_custom_call" | custom-call | tf_op jit(solution)/shard_map/reduce_rows/pallas_call | solution.py:381
  146.6 0.8 slice.11
  147.5 0.6 select_reduce_fusion
  148.1 1.6 %copy.18 = bf16[128,512]{1,0:T(8,128)(2,1)} copy(bf16[128,512]{1,0:T(8,128)(2,1)} %get-tuple-element.33) | data formatting | bytes 262144
  149.7 1.6 %copy.19 = bf16[128,512]{1,0:T(8,128)(2,1)} copy(bf16[128,512]{1,0:T(8,128)(2,1)} %get-tuple-element.34) | data formatting | bytes 262144
  (20 shorter events, 0.0 us)
Async XLA Ops:
  0.6 60.5 %copy-start = (bf16[1,704,1024]{2,1,0:T(8,128)(2,1)S(1)}, bf16[1,704,1024]{2,1,0:T(8,128)(2,1)}, u32[]{:S(2)}) copy-start(bf16[1,704,1024]{2,1,0:T(8,128)(2,1)} %param.15) | copy-start | bytes 4325380
  52.2 3.5 %copy-start.1 = (bf16[16,128,1024]{2,1,0:T(8,128)(2,1)S(1)}, bf16[16,128,1024]{2,1,0:T(8,128)(2,1)}, u32[]{:S(2)}) copy-start(bf16[16,128,1024]{2,1,0:T(8,128)(2,1)} %get-tuple-element.14) | copy-start | bytes 12582916
  55.3 4.2 %copy-start.2 = (bf16[16,64,1024]{2,1,0:T(8,128)(2,1)}, bf16[16,64,1024]{2,1,0:T(8,128)(2,1)S(1)}, u32[]{:S(2)}) copy-start(bf16[16,64,1024]{2,1,0:T(8,128)(2,1)S(1)} %convolution_convert_fusion.4) | copy-start | bytes 6291460
  56.4 1.4 copy-start.7
  57.7 1.7 %copy-start.6 = (bf16[1,704,1024]{2,1,0:T(8,128)(2,1)S(1)}, bf16[1,704,1024]{2,1,0:T(8,128)(2,1)}, u32[]{:S(2)}) copy-start(bf16[1,704,1024]{2,1,0:T(8,128)(2,1)} %param.13) | copy-start | bytes 4325380
  72.4 4.9 %copy-start.3 = (bf16[16,64,1024]{2,1,0:T(8,128)(2,1)S(1)}, bf16[16,64,1024]{2,1,0:T(8,128)(2,1)}, u32[]{:S(2)}) copy-start(bf16[16,64,1024]{2,1,0:T(8,128)(2,1)} %copy-done.2) | copy-start | bytes 6291460
  72.4 4.9 %copy-start.9 = (bf16[1024,704]{0,1:T(8,128)(2,1)S(1)}, bf16[1024,704]{0,1:T(8,128)(2,1)}, u32[]{:S(2)}) copy-start(bf16[1024,704]{0,1:T(8,128)(2,1)} %get-tuple-element.21) | copy-start | bytes 4325380
  77.3 2.8 %copy-start.4 = (bf16[1024,1024]{1,0:T(8,128)(2,1)S(1)}, bf16[1024,1024]{1,0:T(8,128)(2,1)}, u32[]{:S(2)}) copy-start(bf16[1024,1024]{1,0:T(8,128)(2,1)} %get-tuple-element.26) | copy-start | bytes 6291460
  83.3 1.8 %copy-start.8 = (bf16[1,704,1024]{2,1,0:T(8,128)(2,1)S(1)}, bf16[1,704,1024]{2,1,0:T(8,128)(2,1)}, u32[]{:S(2)}) copy-start(bf16[1,704,1024]{2,1,0:T(8,128)(2,1)} %param.14) | copy-start | bytes 4325380
  83.3 1.9 %copy-start.10 = (bf16[1024,704]{0,1:T(8,128)(2,1)S(1)}, bf16[1024,704]{0,1:T(8,128)(2,1)}, u32[]{:S(2)}) copy-start(bf16[1024,704]{0,1:T(8,128)(2,1)} %get-tuple-element.20) | copy-start | bytes 4325380
  90.3 57.2 %copy-start.5 = (s32[128,6]{0,1:T(8,128)S(1)}, s32[128,6]{0,1:T(8,128)}, u32[]{:S(2)}) copy-start(s32[128,6]{0,1:T(8,128)} %param.10) | copy-start | bytes 9220

commit v4 on v3

--- a/solution.py
+++ b/solution.py
@@ -79,8 +79,6 @@
         copy.start()
         sent.append(copy)
 
-    for d in range(1, experts):
-        go(meta, mg.at[me], msend.at[d - 1], mrecv.at[d - 1], peer(expert=(me + d) % experts))
     arrays = ((x, xg), (dy, dyg))
     inner = jnp.minimum(z, outer - 1 - z)
     below_more = z > outer - 1 - z
@@ -155,6 +153,8 @@
         steps += [(at + 2 * n + 9, x_event, (a, n, False)) for n in range(outer - 1)]
         steps += [(at + 2 * n + 11, x_event, (a, n, True)) for n in range(-1, outer - 1)]
     start(0)
+    for d in range(1, experts):
+        go(meta, mg.at[me], msend.at[d - 1], mrecv.at[d - 1], peer(expert=(me + d) % experts))
     for _, run, args in sorted(steps, key=lambda step: step[0]):
         run(*args)
     for a, (s, g) in enumerate(arrays):
@@ -254,9 +254,6 @@
     def arrived(ref, a, i):
         remote(ref, ref, *sems(a, i), cpeer).wait_recv()
 
-    for d in range(1, experts):
-        to = (me + d) % experts
-        go(gate.at[to], gin.at[me], gsend.at[d - 1], grecv.at[d - 1], peer(expert=to))
     for a in range(2):
         for k in range(chunks):
             yy, zz = where(k)
@@ -347,6 +344,9 @@
 
     for k in range(chunks):
         core_step(0, k)
+    for d in range(1, experts):
+        to = (me + d) % experts
+        go(gate.at[to], gin.at[me], gsend.at[d - 1], grecv.at[d - 1], peer(expert=to))
     first_hops(0)
     for k in range(chunks):
         core_step(1, k)

time: 152 us -> 151 us (level)
    pallas_call x1, Pallas kernels: 47.9 us -> 46 us  [gather_all(): pl.pallas_call(functools.partial(gather_kernel, pipes, experts), out_shap...]
where the time goes in v4:
time: 151 us; the launch traced here: 150 us
  Pallas kernels  103 us (68%)
  matrix products  36 us (24%)
  local copies, waits for them, and re-layouts  6.62 us (4%)
  other arithmetic  3.58 us (2%)
    pallas_call x1, Pallas kernels, reduce_all(): pl.pallas_call(functools.partial(reduce_kernel, pipes, experts), out_shap...  57.3 us
    pallas_call x1, Pallas kernels, gather_all(): pl.pallas_call(functools.partial(gather_kernel, pipes, experts), out_shap...  46 us
    dot_general x1, matrix products, body(): grad_up_w = dot(d_up, x, over_rows).astype(BF16)  4.93 us
    dot_general x3, matrix products, select(): lax.dot_general(matrix, source, by_token, preferred_element_type=F32)  4.47 us
    unnamed x24, local copies, waits for them, and re-layouts  4.19 us
    dot_general x1, matrix products, body(): d_act = dot(d_out, down_w, contract)  4.09 us
    dot_general x1, matrix products, body(): partial_out = dot(act, down_w, plain).astype(BF16)  3.4 us
    dot_general x1, matrix products, body(): grad_part = dot(pick, partial_back.reshape(shape), over_slots).astype(BF16)  3.26 us

profile of v4, /device:TPU:9, one launch (start us, length us, event | category | flops | bytes accessed | tf_op | source)
XLA Modules:
  0.0 150.4 jit_solution(6018482574457098037)
XLA Ops:
  0.6 0.0 copy-start
  0.7 0.8 add_convert_fusion.1
  1.5 0.7 convert_element_type.74
  2.2 0.6 maximum_bitcast_fusion.meta
  2.8 46.0 %gather_rows.1 = (bf16[16,128,1024]{2,1,0:T(8,128)(2,1)}, bf16[16,128,1024]{2,1,0:T(8,128)(2,1)}, f32[16,16,128]{2,1,0:T(8,128)}) custom-call(bf16[128,1024]{1,0:T(8,128)(2,1)} %x.1, bf16[128,1024]{1,0:T(8,128)(2,1)} %dy.1, f32[16,128]{1,0:T(8,128)} %maximum_bitcast_fusion.meta), custom_call_target="tpu_custom_call" | custom-call | tf_op jit(solution)/shard_map/gather_rows/pallas_call | solution.py:182
  48.8 0.9 fusion.19
  49.7 0.6 fusion.1
  50.3 3.0 %convolution_convert_fusion.4 = bf16[16,64,1024]{2,1,0:T(8,128)(2,1)S(1)} fusion(bf16[16,64,128]{2,1,0:T(8,128)(2,1)S(1)} %get-tuple-element.19, bf16[16,128,1024]{2,1,0:T(8,128)(2,1)} %get-tuple-element.13), kind=kOutput, calls=%fused_computation.16 | convolution fusion | flops 269484032 | bytes 6553600 | tf_op jit(solution)/shard_map/dot_general | solution.py:434
  53.4 0.4 copy-done.1
  53.8 0.7 convolution_convert_fusion.3
  54.5 0.0 copy-start.7
  54.5 0.7 convolution_convert_fusion.2
  55.2 0.6 copy-done.7
  55.9 1.7 %fusion.11 = f32[1024,704]{0,1:T(8,128)S(1)} fusion(bf16[1024,1024]{1,0:T(8,128)(2,1)S(1)} %bitcast.63, bf16[1,704,1024]{2,1,0:T(8,128)(2,1)S(1)} %copy-done.7), kind=kOutput, calls=%fused_computation.28 | convolution fusion | flops 1476395008 | bytes 6422528 | tf_op jit(solution)/shard_map/dot_general | solution.py:446
  57.6 1.7 %fusion.15 = f32[1024,704]{0,1:T(8,128)S(1)} fusion(bf16[1024,1024]{1,0:T(8,128)(2,1)S(1)} %bitcast.64, bf16[1,704,1024]{2,1,0:T(8,128)(2,1)S(1)} %copy-done.6), kind=kOutput, calls=%fused_computation.32 | convolution fusion | flops 1476395008 | bytes 6422528 | tf_op jit(solution)/shard_map/dot_general | solution.py:445
  59.3 4.1 %multiply_convert_fusion = (bf16[1024,704]{0,1:T(8,128)(2,1)}, bf16[1024,704]{0,1:T(8,128)(2,1)}, bf16[1024,704]{0,1:T(8,128)(2,1)S(1)}) fusion(f32[1024,704]{0,1:T(8,128)S(1)} %fusion.15, f32[1024,704]{0,1:T(8,128)S(1)} %fusion.11, bf16[1024,1024]{1,0:T(8,128)(2,1)S(1)} %bitcast.68, bf16[1,704,1024]{2,1,0:T(8,128)(2,1)S(1)} %copy-done), kind=kOutput, calls=%fused_computation.7 | convolution fusion | flops 1487208448 | bytes 13631488 | tf_op jit(solution)/shard_map/dot_general | solution.py:451
  63.4 2.8 %fusion.6 = bf16[1,704,1024]{2,1,0:T(8,128)(2,1)} fusion(bf16[1024,704]{0,1:T(8,128)(2,1)S(1)} %get-tuple-element.22, bf16[1024,1024]{1,0:T(8,128)(2,1)S(1)} %bitcast.69), kind=kOutput, calls=%fused_computation.23 | convolution fusion | flops 1477115904 | bytes 4980736 | tf_op jit(solution)/shard_map/dot_general | solution.py:457
  66.2 3.4 %fusion = (f32[1024]{0:T(1024)S(1)}, bf16[1024,1024]{1,0:T(8,128)(2,1)}) fusion(bf16[16,64,1024]{2,1,0:T(8,128)(2,1)S(1)} %convolution_convert_fusion.2, bf16[1024,704]{0,1:T(8,128)(2,1)S(1)} %get-tuple-element.22, bf16[1,704,1024]{2,1,0:T(8,128)(2,1)S(1)} %copy-done), kind=kOutput, calls=%fused_computation.1 | convolution fusion | flops 1481636864 | bytes 7081984 | tf_op jit(solution)/shard_map/dot_general | solution.py:450
  69.6 0.1 mul.54
  69.6 0.2 multiply_reduce_fusion
  69.8 0.6 broadcast_in_dim.51.gate
  70.5 4.9 %fusion.5 = bf16[1,704,1024]{2,1,0:T(8,128)(2,1)} fusion(bf16[1024,704]{0,1:T(8,128)(2,1)} %get-tuple-element.20, bf16[1024,1024]{1,0:T(8,128)(2,1)} %bitcast.65), kind=kOutput, calls=%fused_computation.22 | convolution fusion | flops 1477115904 | bytes 4980736 | tf_op jit(solution)/shard_map/dot_general | solution.py:456
  75.4 2.8 %fusion.4 = bf16[1,704,1024]{2,1,0:T(8,128)(2,1)} fusion(bf16[1024,704]{0,1:T(8,128)(2,1)S(1)} %copy-done.9, bf16[1024,1024]{1,0:T(8,128)(2,1)S(1)} %bitcast.66), kind=kOutput, calls=%fused_computation.21 | convolution fusion | flops 1477115904 | bytes 4980736 | tf_op jit(solution)/shard_map/dot_general | solution.py:455
  78.2 3.2 %convolution_convert_fusion.1 = bf16[16,128,1024]{2,1,0:T(8,128)(2,1)} fusion(bf16[16,64,1024]{2,1,0:T(8,128)(2,1)S(1)} %bitcast.67, bf16[16,64,128]{2,1,0:T(8,128)(2,1)S(1)} %get-tuple-element.18), kind=kOutput, calls=%fused_computation.13 | convolution fusion | flops 270532608 | bytes 6553600 | tf_op jit(solution)/shard_map/dot_general | solution.py:461
  81.4 1.8 %fusion.13 = f32[1024,1024]{1,0:T(8,128)S(1)} fusion(bf16[1024,704]{0,1:T(8,128)(2,1)S(1)} %copy-done.9, bf16[1,704,1024]{2,1,0:T(8,128)(2,1)S(1)} %copy-done.6), kind=kOutput, calls=%fused_computation.30 | convolution fusion | flops 1476395008 | bytes 7077888 | tf_op jit(solution)/shard_map/dot_general | solution.py:454
  83.3 1.9 %add_convert_fusion = bf16[1024,1024]{1,0:T(8,128)(2,1)S(1)} fusion(f32[1024,1024]{1,0:T(8,128)S(1)} %fusion.13, bf16[1024,704]{0,1:T(8,128)(2,1)S(1)} %copy-done.10, bf16[1,704,1024]{2,1,0:T(8,128)(2,1)S(1)} %copy-done.8), kind=kOutput, calls=%fused_computation.2 | convolution fusion | flops 1478492160 | bytes 9175040 | tf_op jit(solution)/shard_map/dot_general | solution.py:454
  85.2 3.3 %convolution_convert_fusion = bf16[16,128,1024]{2,1,0:T(8,128)(2,1)} fusion(bf16[16,64,128]{2,1,0:T(8,128)(2,1)S(1)} %get-tuple-element.19, bf16[16,64,1024]{2,1,0:T(8,128)(2,1)S(1)} %bitcast.70), kind=kOutput, calls=%fused_computation.12 | convolution fusion | flops 270532608 | bytes 6553600 | tf_op jit(solution)/shard_map/dot_general | solution.py:462
  88.5 57.3 %reduce_rows.1 = (bf16[128,512]{1,0:T(8,128)(2,1)}, bf16[128,512]{1,0:T(8,128)(2,1)}, f32[16,8,128]{2,1,0:T(8,128)}) custom-call(bf16[4,2,2,128,1024]{4,3,2,1,0:T(8,128)(2,1)} %bitcast.61, bf16[4,2,2,128,1024]{4,3,2,1,0:T(8,128)(2,1)} %bitcast.62, f32[16,8,128]{2,1,0:T(8,128)} %broadcast_in_dim.51.gate), custom_call_target="tpu_custom_call" | custom-call | tf_op jit(solution)/shard_map/reduce_rows/pallas_call | solution.py:381
  145.8 0.8 slice.11
  146.6 0.6 select_reduce_fusion
  147.2 1.6 %copy.18 = bf16[128,512]{1,0:T(8,128)(2,1)} copy(bf16[128,512]{1,0:T(8,128)(2,1)} %get-tuple-element.33) | data formatting | bytes 262144
  148.8 1.6 %copy.19 = bf16[128,512]{1,0:T(8,128)(2,1)} copy(bf16[128,512]{1,0:T(8,128)(2,1)} %get-tuple-element.34) | data formatting | bytes 262144
  (20 shorter events, 0.0 us)
Async XLA Ops:
  0.6 58.7 %copy-start = (bf16[1,704,1024]{2,1,0:T(8,128)(2,1)S(1)}, bf16[1,704,1024]{2,1,0:T(8,128)(2,1)}, u32[]{:S(2)}) copy-start(bf16[1,704,1024]{2,1,0:T(8,128)(2,1)} %param.15) | copy-start | bytes 4325380
  50.3 3.5 %copy-start.1 = (bf16[16,128,1024]{2,1,0:T(8,128)(2,1)S(1)}, bf16[16,128,1024]{2,1,0:T(8,128)(2,1)}, u32[]{:S(2)}) copy-start(bf16[16,128,1024]{2,1,0:T(8,128)(2,1)} %get-tuple-element.14) | copy-start | bytes 12582916
  53.4 4.2 %copy-start.2 = (bf16[16,64,1024]{2,1,0:T(8,128)(2,1)}, bf16[16,64,1024]{2,1,0:T(8,128)(2,1)S(1)}, u32[]{:S(2)}) copy-start(bf16[16,64,1024]{2,1,0:T(8,128)(2,1)S(1)} %convolution_convert_fusion.4) | copy-start | bytes 6291460
  54.5 1.4 copy-start.7
  55.9 1.7 %copy-start.6 = (bf16[1,704,1024]{2,1,0:T(8,128)(2,1)S(1)}, bf16[1,704,1024]{2,1,0:T(8,128)(2,1)}, u32[]{:S(2)}) copy-start(bf16[1,704,1024]{2,1,0:T(8,128)(2,1)} %param.13) | copy-start | bytes 4325380
  70.5 4.9 %copy-start.3 = (bf16[16,64,1024]{2,1,0:T(8,128)(2,1)S(1)}, bf16[16,64,1024]{2,1,0:T(8,128)(2,1)}, u32[]{:S(2)}) copy-start(bf16[16,64,1024]{2,1,0:T(8,128)(2,1)} %copy-done.2) | copy-start | bytes 6291460
  70.5 4.9 %copy-start.9 = (bf16[1024,704]{0,1:T(8,128)(2,1)S(1)}, bf16[1024,704]{0,1:T(8,128)(2,1)}, u32[]{:S(2)}) copy-start(bf16[1024,704]{0,1:T(8,128)(2,1)} %get-tuple-element.21) | copy-start | bytes 4325380
  75.4 2.8 %copy-start.4 = (bf16[1024,1024]{1,0:T(8,128)(2,1)S(1)}, bf16[1024,1024]{1,0:T(8,128)(2,1)}, u32[]{:S(2)}) copy-start(bf16[1024,1024]{1,0:T(8,128)(2,1)} %get-tuple-element.26) | copy-start | bytes 6291460
  81.4 1.8 %copy-start.8 = (bf16[1,704,1024]{2,1,0:T(8,128)(2,1)S(1)}, bf16[1,704,1024]{2,1,0:T(8,128)(2,1)}, u32[]{:S(2)}) copy-start(bf16[1,704,1024]{2,1,0:T(8,128)(2,1)} %param.14) | copy-start | bytes 4325380
  81.4 1.9 %copy-start.10 = (bf16[1024,704]{0,1:T(8,128)(2,1)S(1)}, bf16[1024,704]{0,1:T(8,128)(2,1)}, u32[]{:S(2)}) copy-start(bf16[1024,704]{0,1:T(8,128)(2,1)} %get-tuple-element.20) | copy-start | bytes 4325380
  88.4 58.2 %copy-start.5 = (s32[128,6]{0,1:T(8,128)S(1)}, s32[128,6]{0,1:T(8,128)}, u32[]{:S(2)}) copy-start(s32[128,6]{0,1:T(8,128)} %param.10) | copy-start | bytes 9220
